TPU v7x, 32 devices: a whole 2x2x4 slice. The times are simulated.
32 devices in a mesh: row: 8 (over y, x, core), blk: 4 (over z).
Axes of the slice: x: 2, y: 2, z: 4, core: 2. Of those that a mesh axis runs over, the one named last changes fastest.
Arguments:
- values: bfloat16 [512, 16, 256, 256], P('row', 'blk'), may hold values from -6 to 6
- scales: bfloat16 [512, 16], P('row', 'blk'), may hold values from 0.0049743652 to 0.049804688
- pattern: int32 [512, 16], P('row', 'blk'), may hold values from 0 to 2047, as said below
- omega: bfloat16 [2048, 256, 128], P(('row', 'blk')), may hold values from -6 to 6
Outputs:
- basis: float32 [2048, 256, 128], P(('row', 'blk'))
- upper: float32 [128, 128], replicated
Inputs may be any that keep to these rules, and one draw needn't show every extreme that they name: `pattern`: A block-row of group g = r // 64 has all its column blocks in g * 256 to (g + 1) * 256 - 1. Among the 256 blocks of one device (its block-rows and its positions), at most 64 lie in one aligned run of 64 column blocks, and some run holds exactly 64.
All inputs are finite; a program needn't handle non-finite values.
Results may differ from a plain program's by a relative error of at most 0.0003.
Values may be sent and summed in bfloat16 or wider, within the bound.
A program may use at most 192 MiB of HBM per device.

v0:
```python
import functools

import jax
import jax.numpy as jnp
from jax import lax
from jax.experimental import pallas as pl
from jax.experimental.pallas import tpu as pltpu
from jax.sharding import PartitionSpec as P

MESH = pl.DeviceIdType.MESH
LEVELS = 32767.0
TINY = 1e-30
HOP = 2
ANY = pl.BlockSpec(memory_space=pl.ANY)
SMEM = pl.BlockSpec(memory_space=pltpu.SMEM)


def divisor(n, most):
    return max(d for d in range(1, most + 1) if n % d == 0)


def diagonal(height, width):
    shape = (height, width)
    return lax.broadcasted_iota(jnp.int32, shape, 0) == lax.broadcasted_iota(jnp.int32, shape, 1)


def encode(x, eye):
    peak = jnp.max(jnp.abs(x), axis=2, keepdims=True)
    live = peak > TINY
    inverse = jnp.where(live, LEVELS / jnp.where(live, peak, 1.0), 0.0)
    code = jnp.round(x * inverse).astype(jnp.int32).astype(jnp.int16)
    step = jnp.sum(jnp.where(eye[None], peak * (1.0 / LEVELS), 0.0), axis=1, keepdims=True)
    return code, step


def decode(code, step, eye):
    column = jnp.sum(jnp.where(eye[None], step, 0.0), axis=2, keepdims=True)
    return code.astype(jnp.int32).astype(jnp.float32) * column


def greet(me, n):
    barrier = pltpu.get_barrier_semaphore()

    @pl.when(me > 0)
    def _():
        pl.semaphore_signal(barrier, inc=1, device_id={"blk": me - 1}, device_id_type=MESH)

    @pl.when(me < n - 1)
    def _():
        pl.semaphore_signal(barrier, inc=1, device_id={"blk": me + 1}, device_id_type=MESH)

    peers = jnp.where(me > 0, 1, 0) + jnp.where(me < n - 1, 1, 0)
    pl.semaphore_wait(barrier, peers)


def gather_steps(me, n, own_ref, slab_ref, send_sem, recv_sem):
    blocks = own_ref.shape[0]
    pieces = send_sem.shape[2]
    size = blocks // pieces

    def copy(way, t, c, owner):
        src = slab_ref.at[pl.ds(owner * blocks + c * size, size)]
        return pltpu.make_async_remote_copy(
            src_ref=src,
            dst_ref=src,
            send_sem=send_sem.at[way, t, c],
            recv_sem=recv_sem.at[way, t, c],
            device_id={"blk": me + 1 - 2 * way},
            device_id_type=MESH,
        )

    def first(way, c):
        return pltpu.make_async_remote_copy(
            src_ref=own_ref.at[pl.ds(c * size, size)],
            dst_ref=slab_ref.at[pl.ds(me * blocks + c * size, size)],
            send_sem=send_sem.at[way, 0, c],
            recv_sem=recv_sem.at[way, 0, c],
            device_id={"blk": me + 1 - 2 * way},
            device_id_type=MESH,
        )

    def has(way, t):
        behind = me if way == 0 else n - 1 - me
        return behind >= t

    def goes(way):
        return me < n - 1 if way == 0 else me > 0

    def owner_of(way, t):
        return me - t if way == 0 else me + t

    def step(v):
        t = v // pieces
        c = v % pieces
        for way in (0, 1):

            @pl.when((t == 0) & goes(way))
            def _(way=way):
                first(way, c).start()

            @pl.when((t > 0) & has(way, t))
            def _(way=way):
                copy(way, t - 1, c, owner_of(way, t)).wait_recv()

            @pl.when((t > 0) & (t < n - 1) & has(way, t) & goes(way))
            def _(way=way):
                copy(way, t, c, owner_of(way, t)).start()

    def finish():
        @pl.loop(0, (n - 1) * pieces)
        def _(v):
            t = v // pieces
            c = v % pieces
            for way in (0, 1):

                @pl.when(has(way, t) & goes(way))
                def _(way=way):
                    copy(way, t, c, me).wait_send()

    return step, n * pieces, finish


def gather(own, n, part):
    blocks = own.shape[0]
    pieces = divisor(blocks, 8)

    def body(own_ref, slab_ref, send_sem, recv_sem):
        me = lax.axis_index("blk")
        greet(me, n)
        step, steps, finish = gather_steps(me, n, own_ref, slab_ref, send_sem, recv_sem)
        pl.loop(0, steps)(step)
        finish()

    return pl.pallas_call(
        body,
        out_shape=jax.ShapeDtypeStruct((n * blocks,) + own.shape[1:], own.dtype),
        in_specs=[ANY],
        out_specs=ANY,
        scratch_shapes=[pltpu.SemaphoreType.DMA((2, n - 1, pieces))] * 2,
        compiler_params=pltpu.CompilerParams(collective_id=1 + part, has_side_effects=True),
        name=f"gather_{part}",
    )(own)


def products(values, own, slab, cols, weights, prev, last, n, part):
    rows, per, side, _ = values.shape
    blocks, wide, _ = own.shape
    lanes = 128
    items = rows * per
    columns = n * blocks
    batch = divisor(rows, 4)
    pieces = rows // batch
    lag = HOP * (n - 1)
    slots = lag + 2
    out_batch = divisor(columns, 8)

    def body(
        cols_ref, weights_ref, prev_ref, last_ref, values_ref, own_ref, slab_ref, z_ref,
        slab, ring, part_ref, in_code, in_step, out_code, out_step, sums, stage,
        slab_sem, ring_sem, stage_sem, send_sem, recv_sem,
    ):
        me = lax.axis_index("blk")
        eye = diagonal(wide, lanes)

        def load(c):
            slot = c % slots
            return pltpu.make_async_copy(
                values_ref.at[pl.ds(c * batch, batch)], ring.at[slot], ring_sem.at[slot]
            )

        def shard(d, src):
            return pltpu.make_async_copy(src, slab.at[pl.ds(d * blocks, blocks)], slab_sem.at[d])

        load(0).start()
        for d in range(n):

            @pl.when(me == d)
            def _(d=d):
                shard(d, own_ref).start()

            @pl.when(me != d)
            def _(d=d):
                shard(d, slab_ref.at[pl.ds(d * blocks, blocks)]).start()

        greet(me, n)
        sums[items] = jnp.zeros((wide, side), jnp.float32)

        @pl.when(me == 0)
        def _():
            in_step[0] = jnp.zeros((rows, 1, lanes), jnp.float32)

        @pl.when(me == n - 1)
        def _():
            in_step[1] = jnp.zeros((rows, 1, lanes), jnp.float32)

        for d in range(n):
            shard(d, own_ref).wait()

        def copies(way, c):
            to = {"blk": me + 1 - 2 * way}
            at = pl.ds(c * batch, batch)
            return [
                pltpu.make_async_remote_copy(
                    src_ref=src.at[way, at],
                    dst_ref=dst.at[way, at],
                    send_sem=send_sem.at[way, kind, c],
                    recv_sem=recv_sem.at[way, kind, c],
                    device_id=to,
                    device_id_type=MESH,
                )
                for kind, (src, dst) in enumerate(((out_code, in_code), (out_step, in_step)))
            ]

        def incoming(way, c):
            at = pl.ds(c * batch, batch)
            return decode(in_code[way, at], in_step[way, at], eye)

        def relay(way, c, has, goes):
            @pl.when((c >= 0) & (c < pieces) & has)
            def _():
                for one in copies(way, c):
                    one.wait_recv()

            @pl.when((c >= 0) & (c < pieces) & goes)
            def _():
                at = pl.ds(c * batch, batch)
                code, step = encode(part_ref[at] + incoming(way, c), eye)
                out_code[way, at] = code
                out_step[way, at] = step
                for one in copies(way, c):
                    one.start()

        @pl.loop(0, pieces + lag)
        def _(s):
            @pl.when(s + 1 < pieces)
            def _():
                load(s + 1).start()

            @pl.when(s < pieces)
            def _():
                load(s).wait()
                for r in range(batch):
                    total = None
                    for k in range(per):
                        at = (s * batch + r) * per + k
                        term = weights_ref[at] * lax.dot_general(
                            slab[cols_ref[at]],
                            ring[s % slots, r, k],
                            (((1,), (1,)), ((), ())),
                            preferred_element_type=jnp.float32,
                        )
                        total = term if total is None else total + term
                    part_ref[s * batch + r] = total

            relay(0, s - HOP * me, me > 0, me < n - 1)
            relay(1, s - HOP * (n - 1 - me), me < n - 1, me > 0)
            c = s - lag

            @pl.when(c >= 0)
            def _():
                total = part_ref[pl.ds(c * batch, batch)] + incoming(0, c) + incoming(1, c)
                high = total.astype(jnp.bfloat16)
                low = (total - high.astype(jnp.float32)).astype(jnp.bfloat16)
                for r in range(batch):
                    both = jnp.concatenate([high[r], low[r]], axis=0)
                    for k in range(per):
                        at = (c * batch + r) * per + k
                        pair = lax.dot_general(
                            both,
                            ring[c % slots, r, k],
                            (((1,), (0,)), ((), ())),
                            preferred_element_type=jnp.float32,
                        )
                        term = weights_ref[at] * (pair[:wide] + pair[wide:])
                        sums[at] = term + sums[prev_ref[at]]

        @pl.loop(0, pieces)
        def _(c):
            @pl.when(me < n - 1)
            def _():
                for one in copies(0, c):
                    one.wait_send()

            @pl.when(me > 0)
            def _():
                for one in copies(1, c):
                    one.wait_send()

        def store(i):
            return pltpu.make_async_copy(
                stage.at[i % 2], z_ref.at[pl.ds(i * out_batch, out_batch)], stage_sem.at[i % 2]
            )

        count = columns // out_batch

        @pl.loop(0, count)
        def _(i):
            @pl.when(i >= 2)
            def _():
                store(i - 2).wait()

            for u in range(out_batch):
                stage[i % 2, u] = sums[last_ref[i * out_batch + u]]
            store(i).start()

        for i in range(max(count - 2, 0), count):
            store(i).wait()

    f32 = jnp.float32
    return pl.pallas_call(
        body,
        out_shape=jax.ShapeDtypeStruct((columns, wide, side), f32),
        in_specs=[SMEM] * 4 + [ANY] * 3,
        out_specs=ANY,
        scratch_shapes=[
            pltpu.VMEM((columns, wide, side), own.dtype),
            pltpu.VMEM((slots, batch, per, side, side), values.dtype),
            pltpu.VMEM((rows, wide, side), f32),
            pltpu.VMEM((2, rows, wide, side), jnp.int16),
            pltpu.VMEM((2, rows, 1, lanes), f32),
            pltpu.VMEM((2, rows, wide, side), jnp.int16),
            pltpu.VMEM((2, rows, 1, lanes), f32),
            pltpu.VMEM((items + 1, wide, side), f32),
            pltpu.VMEM((2, out_batch, wide, side), f32),
            pltpu.SemaphoreType.DMA((n,)),
            pltpu.SemaphoreType.DMA((slots,)),
            pltpu.SemaphoreType.DMA((2,)),
            pltpu.SemaphoreType.DMA((2, 2, pieces)),
            pltpu.SemaphoreType.DMA((2, 2, pieces)),
        ],
        compiler_params=pltpu.CompilerParams(
            collective_id=8 + part, has_side_effects=True, vmem_limit_bytes=62 << 20
        ),
        name=f"products_{part}",
    )(cols, weights, prev, last, values, own, slab)


def scatter(z, n, part, own=None):
    columns, wide, side = z.shape
    lanes = 128
    blocks = columns // n
    pieces = divisor(blocks, 8)
    size = blocks // pieces
    reach = (n - 1) * pieces
    total_steps = max(reach + HOP, pieces + HOP * (n - 1))
    fused = own is not None
    if fused:
        total_steps = max(total_steps, n * pieces)

    def body(*refs):
        if fused:
            z_ref, own_ref, out_ref, slab_ref = refs[:4]
            refs = refs[4:]
            gather_send, gather_recv = refs[-2:]
        else:
            z_ref, out_ref = refs[:2]
            refs = refs[2:]
        (zs, mine, in_code, in_step, out_code, out_step, z_sem, mine_sem, send_sem, recv_sem) = refs[:10]
        me = lax.axis_index("blk")
        eye = diagonal(wide, lanes)

        def spot(way, u):
            d = n - 1 - u // pieces if way == 0 else u // pieces
            return pl.ds(d * blocks + u % pieces * size, size)

        def load(way, u):
            at = spot(way, u)
            return pltpu.make_async_copy(z_ref.at[at], zs.at[at], z_sem.at[way, u])

        mine_copy = pltpu.make_async_copy(z_ref.at[pl.ds(me * blocks, blocks)], mine, mine_sem)
        far = ((n - 1 - me) * pieces, me * pieces)

        @pl.loop(0, reach)
        def _(u):
            for way in (0, 1):

                @pl.when(u < far[way])
                def _(way=way):
                    load(way, u).start()

        mine_copy.start()
        greet(me, n)

        def copies(way, u):
            here = pl.ds(u * size, size)
            to = {"blk": me + 1 - 2 * way}
            return [
                pltpu.make_async_remote_copy(
                    src_ref=src.at[way, here],
                    dst_ref=dst.at[way, here],
                    send_sem=send_sem.at[way, kind, u],
                    recv_sem=recv_sem.at[way, kind, u],
                    device_id=to,
                    device_id_type=MESH,
                )
                for kind, (src, dst) in enumerate(((out_code, in_code), (out_step, in_step)))
            ]

        def incoming(way, u):
            here = pl.ds(u * size, size)
            return decode(in_code[way, here], in_step[way, here], eye)

        def push(way, u, value):
            here = pl.ds(u * size, size)
            code, step = encode(value, eye)
            out_code[way, here] = code
            out_step[way, here] = step
            for one in copies(way, u):
                one.start()

        if fused:
            step, steps, finish = gather_steps(me, n, own_ref, slab_ref, gather_send, gather_recv)

        mine_copy.wait()

        @pl.loop(0, total_steps)
        def _(s):
            if fused:

                @pl.when(s < steps)
                def _():
                    step(s)

            for way in (0, 1):
                behind = me if way == 0 else n - 1 - me
                u = s - HOP * behind
                inside = (u >= 0) & (u < far[way])

                @pl.when(inside)
                def _(way=way, u=u):
                    load(way, u).wait()

                @pl.when(inside & (behind == 0))
                def _(way=way, u=u):
                    push(way, u, zs[spot(way, u)])

                @pl.when(inside & (behind > 0))
                def _(way=way, u=u):
                    for one in copies(way, u):
                        one.wait_recv()
                    push(way, u, zs[spot(way, u)] + incoming(way, u))

                @pl.when((behind > 0) & (u >= far[way]) & (u < far[way] + pieces))
                def _(way=way, u=u):
                    for one in copies(way, u):
                        one.wait_recv()
                    at = pl.ds((u - far[way]) * size, size)
                    mine[at] = mine[at] + incoming(way, u)

        result = pltpu.make_async_copy(mine, out_ref, mine_sem)
        result.start()

        @pl.loop(0, reach)
        def _(u):
            for way in (0, 1):

                @pl.when(u < far[way])
                def _(way=way):
                    for one in copies(way, u):
                        one.wait_send()

        if fused:
            finish()
        result.wait()

    f32 = jnp.float32
    scratch = [
        pltpu.VMEM((columns, wide, side), f32),
        pltpu.VMEM((blocks, wide, side), f32),
        pltpu.VMEM((2, reach * size, wide, side), jnp.int16),
        pltpu.VMEM((2, reach * size, 1, lanes), f32),
        pltpu.VMEM((2, reach * size, wide, side), jnp.int16),
        pltpu.VMEM((2, reach * size, 1, lanes), f32),
        pltpu.SemaphoreType.DMA((2, reach)),
        pltpu.SemaphoreType.DMA(()),
        pltpu.SemaphoreType.DMA((2, 2, reach)),
        pltpu.SemaphoreType.DMA((2, 2, reach)),
    ]
    out_shape = [jax.ShapeDtypeStruct((blocks, wide, side), f32)]
    args = [z]
    if fused:
        args.append(own)
        out_shape.append(jax.ShapeDtypeStruct((columns,) + own.shape[1:], own.dtype))
        scratch += [pltpu.SemaphoreType.DMA((2, n - 1, divisor(blocks, 8)))] * 2
    return pl.pallas_call(
        body,
        out_shape=out_shape,
        in_specs=[ANY] * len(args),
        out_specs=[ANY] * len(out_shape),
        scratch_shapes=scratch,
        compiler_params=pltpu.CompilerParams(
            collective_id=16 + part, has_side_effects=True, vmem_limit_bytes=62 << 20
        ),
        name=f"scatter_{part}",
    )(*args)


def all_sum(x, axis):
    n = lax.axis_size(axis)
    if n & (n - 1):
        return lax.psum(x, axis)
    bit = 1
    while bit < n:
        x = x + lax.ppermute(x, axis, [(i, i ^ bit) for i in range(n)])
        bit *= 2
    return x


def gram_of(z):
    blocks, width, side = z.shape
    batch = divisor(blocks, 8)

    def body(z_ref, out_ref):
        @pl.when(pl.program_id(0) == 0)
        def _():
            out_ref[...] = jnp.zeros_like(out_ref)

        for b in range(batch):
            out_ref[...] += lax.dot_general(
                z_ref[b],
                z_ref[b],
                (((1,), (1,)), ((), ())),
                precision=lax.Precision.HIGHEST,
                preferred_element_type=jnp.float32,
            )

    return pl.pallas_call(
        body,
        out_shape=jax.ShapeDtypeStruct((width, width), jnp.float32),
        grid=(blocks // batch,),
        in_specs=[pl.BlockSpec((batch, width, side), lambda i: (i, 0, 0))],
        out_specs=pl.BlockSpec((width, width), lambda i: (0, 0)),
        name="gram",
    )(z)


def solve(z, inverse):
    blocks, width, side = z.shape
    batch = divisor(blocks, 8)

    def body(z_ref, inverse_ref, out_ref):
        for b in range(batch):
            out_ref[b] = lax.dot_general(
                z_ref[b],
                inverse_ref[...],
                (((0,), (1,)), ((), ())),
                precision=lax.Precision.HIGHEST,
                preferred_element_type=jnp.float32,
            )

    return pl.pallas_call(
        body,
        out_shape=jax.ShapeDtypeStruct((blocks, side, width), jnp.float32),
        grid=(blocks // batch,),
        in_specs=[
            pl.BlockSpec((batch, width, side), lambda i: (i, 0, 0)),
            pl.BlockSpec((width, width), lambda i: (0, 0)),
        ],
        out_specs=pl.BlockSpec((batch, side, width), lambda i: (i, 0, 0)),
        name="solve",
    )(z, inverse)


def local(values, scales, pattern, omega):
    rows, per = pattern.shape
    blocks, side, width = omega.shape
    n = lax.axis_size("blk")
    items = rows * per
    columns = blocks * n
    cols = pattern.reshape(-1) - lax.axis_index("row") * columns
    weights = scales.astype(jnp.float32).reshape(-1)
    slot = jnp.arange(items)
    same = cols[:, None] == cols[None, :]
    prev = jnp.max(jnp.where(same & (slot[None, :] < slot[:, None]), slot[None, :], -1), axis=1)
    prev = jnp.where(prev < 0, items, prev)
    hits = jnp.arange(columns)[:, None] == cols[None, :]
    last = jnp.max(jnp.where(hits, slot[None, :], -1), axis=1)
    last = jnp.where(last < 0, items, last)

    parts = 2
    wide = width // parts
    turned = jnp.transpose(omega, (0, 2, 1)).reshape(blocks, parts, wide, side)
    own = [turned[:, p] for p in range(parts)]
    slab = gather(own[0], n, 0)
    sums = []
    for p in range(parts):
        z = products(values, own[p], slab, cols, weights, prev, last, n, p)
        if p + 1 < parts:
            piece, slab = scatter(z, n, p, own[p + 1])
        else:
            (piece,) = scatter(z, n, p)
        sums.append(piece)
    flat = jnp.concatenate(sums, axis=1)

    total_rows = columns * side * lax.axis_size("row")
    gram = all_sum(all_sum(gram_of(flat), "row"), "blk") / total_rows
    lower = jnp.linalg.cholesky(gram)
    inverse = jax.scipy.linalg.solve_triangular(lower, jnp.eye(width, dtype=jnp.float32), lower=True)
    return solve(flat, inverse), lower.T


def solution(mesh):
    return jax.shard_map(
        local,
        mesh=mesh,
        in_specs=(
            P("row", "blk", None, None),
            P("row", "blk"),
            P("row", "blk"),
            P(("row", "blk"), None, None),
        ),
        out_specs=(P(("row", "blk"), None, None), P()),
        check_vma=False,
    )
```

profile of v0, /device:TPU:0, one launch (start us, length us, event | category | flops | bytes accessed | tf_op | source)
XLA Modules:
  0.0 747.4 jit_solution(5884933338872810303)
XLA Ops:
  0.6 0.7 broadcast_subtract_fusion
  1.4 0.1 sub.10.cols_ref
  1.5 0.2 select_reduce_fusion
  1.7 0.8 copy.20
  2.5 0.7 reshape.39.weights_ref
  3.2 6.4 copy.21
  9.6 4.8 slice_bitcast_fusion.1
  14.4 141.1 %gather_0.1.slab_ref = bf16[256,64,256]{2,1,0:T(8,128)(2,1)} custom-call(bf16[64,64,256]{2,1,0:T(8,128)(2,1)} %get-tuple-element.14.own_ref), custom_call_target="tpu_custom_call" | custom-call | tf_op jit(solution)/shard_map/gather_0/pallas_call | solution.py:134
  155.5 0.6 compare_select_fusion
  156.1 79.0 %products_0.1.refs_0_ = f32[256,64,256]{2,1,0:T(8,128)} custom-call(s32[256]{0:T(256)} %copy-done, f32[256]{0:T(256)} %reshape.39.weights_ref, s32[256]{0:T(256)} %get-tuple-element.19.prev_ref, s32[256]{0:T(256)} %get-tuple-element.18.last_ref, bf16[64,4,256,256]{3,2,1,0:T(8,128)(2,1)} %values_ref.3, bf16[64,64,256]{2,1,0:T(8,128)(2,1)} %get-tuple-element.14.own_ref, ...), custom_call_target="tpu_custom_call" | custom-call | tf_op jit(solution)/shard_map/products_0/pallas_call | solution.py:310
  235.1 213.1 %scatter_0.1 = (f32[64,64,256]{2,1,0:T(8,128)}, bf16[256,64,256]{2,1,0:T(8,128)(2,1)}) custom-call(f32[256,64,256]{2,1,0:T(8,128)} %products_0.1.refs_0_, bf16[64,64,256]{2,1,0:T(8,128)(2,1)} %get-tuple-element.15.refs_1_.own_ref), custom_call_target="tpu_custom_call" | custom-call | tf_op jit(solution)/shard_map/scatter_0/pallas_call | solution.py:485
  448.2 78.2 %products_1.1.refs_0_ = f32[256,64,256]{2,1,0:T(8,128)} custom-call(s32[256]{0:T(256)} %copy-done, f32[256]{0:T(256)} %reshape.39.weights_ref, s32[256]{0:T(256)} %get-tuple-element.19.prev_ref, s32[256]{0:T(256)} %get-tuple-element.18.last_ref, bf16[64,4,256,256]{3,2,1,0:T(8,128)(2,1)} %values_ref.3, ...), custom_call_target="tpu_custom_call" | custom-call | tf_op jit(solution)/shard_map/products_1/pallas_call | solution.py:310
  526.4 142.3 %scatter_1.1 = f32[64,64,256]{2,1,0:T(8,128)} custom-call(f32[256,64,256]{2,1,0:T(8,128)} %products_1.1.refs_0_), custom_call_target="tpu_custom_call" | custom-call | tf_op jit(solution)/shard_map/scatter_1/pallas_call | solution.py:485
  668.7 7.7 %pad_maximum_fusion.z_ref = f32[64,128,256]{2,1,0:T(8,128)} fusion(f32[64,64,256]{2,1,0:T(8,128)} %scatter_1.1, f32[64,64,256]{2,1,0:T(8,128)} %get-tuple-element.4), kind=kLoop, calls=%fused_computation | loop fusion | flops 2097152 | bytes 16777216 | tf_op jit(solution)/shard_map/concatenate | solution.py:593
  676.4 10.8 %gram.1 = f32[128,128]{1,0:T(8,128)} custom-call(f32[64,128,256]{2,1,0:T(8,128)} %pad_maximum_fusion.z_ref), custom_call_target="tpu_custom_call" | custom-call | tf_op jit(solution)/shard_map/gram/pallas_call | solution.py:527
  687.2 0.9 copy.25
  688.2 1.2 collective-permute-done
  689.5 1.6 collective-permute-start.1
  691.0 2.8 collective-permute-done.1
  693.8 1.6 collective-permute-start.2
  695.4 2.7 collective-permute-done.2
  698.1 4.6 collective-permute-start.3
  702.8 2.2 collective-permute-done.3
  705.0 1.2 collective-permute-start.4
  706.2 4.1 collective-permute-done.4
  710.4 11.7 %cholesky.17 = f32[128,128]{1,0:T(8,128)S(1)} custom-call(f32[128,128]{1,0:T(8,128)S(1)} %fusion.3), custom_call_target="Cholesky" | custom-call | tf_op jit(solution)/shard_map/jit(cholesky)/cholesky | solution.py:597
  722.1 0.6 compare_reduce_fusion
  722.8 0.7 fusion.4
  723.5 0.7 copy.27
  724.2 9.8 %custom-call.7 = f32[1,128,128]{1,2,0:T(8,128)S(1)} custom-call(f32[1,128,128]{2,1,0:T(8,128)S(1)} %get-tuple-element.17), custom_call_target="InvertDiagBlocksLowerTriangular" | custom-call | tf_op jit(solution)/shard_map/jit(_solve_triangular)/triangular_solve | solution.py:598
  734.0 0.9 fusion.1.inverse_ref
  734.9 12.5 %solve.1 = f32[64,256,128]{2,1,0:T(8,128)} custom-call(f32[64,128,256]{2,1,0:T(8,128)} %pad_maximum_fusion.z_ref, f32[128,128]{1,0:T(8,128)} %fusion.1.inverse_ref), custom_call_target="tpu_custom_call" | custom-call | tf_op jit(solution)/shard_map/solve/pallas_call | solution.py:551
  (12 shorter events, 0.4 us)
Async XLA Ops:
  1.5 8.1 %copy-start = (s32[256]{0:T(256)}, s32[256]{0:T(256)S(1)}, u32[]{:S(2)}) copy-start(s32[256]{0:T(256)S(1)} %sub.10.cols_ref) | copy-start | bytes 3076
  688.1 1.3 collective-permute-start
  689.5 4.3 collective-permute-start.1
  693.8 4.3 collective-permute-start.2
  698.1 6.9 collective-permute-start.3
  705.0 5.2 collective-permute-start.4
where the time goes:
time: 748 us; the launch traced here: 747 us
  Pallas kernels  677 us (91%)
  other arithmetic  32.1 us (4%)
  local copies, waits for them, and re-layouts  14.6 us (2%)
  waiting for transfers between devices  13.1 us (2%)
  starting transfers between devices  9.01 us (1%)
    pallas_call x2, Pallas kernels, scatter(): pl.pallas_call(body, out_shape=out_shape, in_specs=[ANY] * len(args), out...  355 us
    pallas_call x2, Pallas kernels, products(): pl.pallas_call(body, out_shape=jax.ShapeDtypeStruct((columns, wide, side)...  157 us
    pallas_call x1, Pallas kernels, gather(): pl.pallas_call(body, out_shape=jax.ShapeDtypeStruct((n * blocks,) + own.s...  141 us
  transfers between devices with their start and end apart: 5, of which 5 were waited for; matrix products, arithmetic and copies ran while one was open for 0% of the time, Pallas kernels for 0%

commit v1 on v0

v1 whole, which is shorter than its diff:
```python
import math

import jax
import jax.numpy as jnp
from jax import lax
from jax.experimental import pallas as pl
from jax.experimental.pallas import tpu as pltpu
from jax.sharding import PartitionSpec as P

MESH = pl.DeviceIdType.MESH
LEVELS = 32767.0
TINY = 1e-30
HOP = 2
ANY = pl.BlockSpec(memory_space=pl.ANY)
SMEM = pl.BlockSpec(memory_space=pltpu.SMEM)


def divisor(n, most):
    return max(d for d in range(1, most + 1) if n % d == 0)


def diagonal(height, width):
    shape = (height, width)
    return lax.broadcasted_iota(jnp.int32, shape, 0) == lax.broadcasted_iota(jnp.int32, shape, 1)


def encode(x, eye):
    peak = jnp.max(jnp.abs(x), axis=2, keepdims=True)
    live = peak > TINY
    inverse = jnp.where(live, LEVELS / jnp.where(live, peak, 1.0), 0.0)
    code = jnp.round(x * inverse).astype(jnp.int32).astype(jnp.int16)
    step = jnp.sum(jnp.where(eye[None], peak * (1.0 / LEVELS), 0.0), axis=1, keepdims=True)
    return code, step


def decode(code, step, eye):
    column = jnp.sum(jnp.where(eye[None], step, 0.0), axis=2, keepdims=True)
    return code.astype(jnp.int32).astype(jnp.float32) * column


def greet(me, n):
    barrier = pltpu.get_barrier_semaphore()

    @pl.when(me > 0)
    def _():
        pl.semaphore_signal(barrier, inc=1, device_id={"blk": me - 1}, device_id_type=MESH)

    @pl.when(me < n - 1)
    def _():
        pl.semaphore_signal(barrier, inc=1, device_id={"blk": me + 1}, device_id_type=MESH)

    peers = jnp.where(me > 0, 1, 0) + jnp.where(me < n - 1, 1, 0)
    pl.semaphore_wait(barrier, peers)


def gather_steps(me, n, base, count, size, own_ref, slab_ref, send_sem, recv_sem):
    blocks = own_ref.shape[0]
    pieces = count // size

    def copy(way, t, c, owner):
        here = slab_ref.at[pl.ds(owner * blocks + base + c * size, size)]
        return pltpu.make_async_remote_copy(
            src_ref=here,
            dst_ref=here,
            send_sem=send_sem.at[way, t, c],
            recv_sem=recv_sem.at[way, t, c],
            device_id={"blk": me + 1 - 2 * way},
            device_id_type=MESH,
        )

    def first(way, c):
        return pltpu.make_async_remote_copy(
            src_ref=own_ref.at[pl.ds(base + c * size, size)],
            dst_ref=slab_ref.at[pl.ds(me * blocks + base + c * size, size)],
            send_sem=send_sem.at[way, 0, c],
            recv_sem=recv_sem.at[way, 0, c],
            device_id={"blk": me + 1 - 2 * way},
            device_id_type=MESH,
        )

    def has(way, t):
        behind = me if way == 0 else n - 1 - me
        return behind >= t

    def goes(way):
        return me < n - 1 if way == 0 else me > 0

    def owner_of(way, t):
        return me - t if way == 0 else me + t

    def step(v):
        t = v // pieces
        c = v % pieces
        for way in (0, 1):

            @pl.when((t == 0) & goes(way))
            def _(way=way):
                first(way, c).start()

            @pl.when((t > 0) & has(way, t))
            def _(way=way):
                copy(way, t - 1, c, owner_of(way, t)).wait_recv()

            @pl.when((t > 0) & (t < n - 1) & has(way, t) & goes(way))
            def _(way=way):
                copy(way, t, c, owner_of(way, t)).start()

    def finish():
        @pl.loop(0, (n - 1) * pieces)
        def _(v):
            t = v // pieces
            c = v % pieces
            for way in (0, 1):

                @pl.when(has(way, t) & goes(way))
                def _(way=way):
                    copy(way, t, c, me).wait_send()

    return step, n * pieces, finish


def gather_sems(n, count, size):
    return [pltpu.SemaphoreType.DMA((2, n - 1, count // size))] * 2


def gather(own, n):
    blocks = own.shape[0]
    size = divisor(blocks, 4)

    def body(own_ref, slab_ref, *sems):
        me = lax.axis_index("blk")
        greet(me, n)
        step, steps, finish = gather_steps(me, n, 0, blocks, size, own_ref, slab_ref, *sems)
        pl.loop(0, steps)(step)
        finish()

    return pl.pallas_call(
        body,
        out_shape=jax.ShapeDtypeStruct((n * blocks,) + own.shape[1:], own.dtype),
        in_specs=[ANY],
        out_specs=ANY,
        scratch_shapes=gather_sems(n, blocks, size),
        compiler_params=pltpu.CompilerParams(collective_id=1, has_side_effects=True),
        name="gather",
    )(own)


def reduce_scratch(n, count, size, wide, side, lanes):
    far = (n - 1) * count
    sems = pltpu.SemaphoreType.DMA((2, 2, far // size))
    code = pltpu.VMEM((2, far, wide, side), jnp.int16)
    step = pltpu.VMEM((2, far, 1, lanes), jnp.float32)
    return [code, step, code, step, sems, sems]


def reduce_steps(me, n, count, size, eye, read, total, base, scratch, beside):
    in_code, in_step, out_code, out_step, send_sem, recv_sem = scratch
    pieces = count // size
    reach = (n - 1) * pieces
    far = ((n - 1 - me) * pieces, me * pieces)
    hop = max(pieces, HOP) if beside else HOP
    start = pieces if beside else 0

    def copies(way, u):
        here = pl.ds(u * size, size)
        to = {"blk": me + 1 - 2 * way}
        return [
            pltpu.make_async_remote_copy(
                src_ref=src.at[way, here],
                dst_ref=dst.at[way, here],
                send_sem=send_sem.at[way, kind, u],
                recv_sem=recv_sem.at[way, kind, u],
                device_id=to,
                device_id_type=MESH,
            )
            for kind, (src, dst) in enumerate(((out_code, in_code), (out_step, in_step)))
        ]

    def incoming(way, u):
        here = pl.ds(u * size, size)
        return decode(in_code[way, here], in_step[way, here], eye)

    def push(way, u, value):
        here = pl.ds(u * size, size)
        code, step = encode(value, eye)
        out_code[way, here] = code
        out_step[way, here] = step
        for one in copies(way, u):
            one.start()

    def source(way, u):
        d = n - 1 - u // pieces if way == 0 else u // pieces
        return read(d, u % pieces)

    def step(s):
        for way in (0, 1):
            behind = me if way == 0 else n - 1 - me
            u = s - start - hop * behind
            inside = (u >= 0) & (u < far[way])

            @pl.when(inside & (behind == 0))
            def _(way=way, u=u):
                push(way, u, source(way, u))

            @pl.when(inside & (behind > 0))
            def _(way=way, u=u):
                for one in copies(way, u):
                    one.wait_recv()
                push(way, u, source(way, u) + incoming(way, u))

            @pl.when((behind > 0) & (u >= far[way]) & (u < far[way] + pieces))
            def _(way=way, u=u):
                for one in copies(way, u):
                    one.wait_recv()
                at = pl.ds(base + (u - far[way]) * size, size)
                total[at] = total[at] + incoming(way, u)

    def finish():
        @pl.loop(0, reach)
        def _(u):
            for way in (0, 1):

                @pl.when(u < far[way])
                def _(way=way):
                    for one in copies(way, u):
                        one.wait_send()

    return step, start + max([reach] + [hop * b + (n - b) * pieces for b in range(1, n)]), finish


def stage(part, values, own, slab, tables, n, following=None, rest=None):
    rows, per, side, _ = values.shape
    blocks, wide, _ = own.shape
    lanes = 128
    items = rows * per
    columns = n * blocks
    batch = divisor(rows, 4)
    pieces = rows // batch
    lag = HOP * (n - 1)
    slots = lag + 2
    half = blocks // 2
    late = blocks - half
    now = half if following is not None else blocks
    now_size = divisor(now, 4 if following is not None else 8)
    late_size = divisor(late, 4)
    gather_size = divisor(half, 4)
    f32 = jnp.float32

    args = dict(zip(("cols", "weights", "prev", "last"), tables))
    args.update(values=values, own=own, slab=slab)
    specs = [SMEM] * 4 + [ANY] * 3
    cuts = [(0, half)] + ([(half, blocks)] if following is None else [])
    outs = {
        f"piece{i}": jax.ShapeDtypeStruct((b - a, wide, side), f32) for i, (a, b) in enumerate(cuts)
    }
    scratch = dict(
        held=pltpu.VMEM((columns, wide, side), own.dtype),
        ring=pltpu.VMEM((slots, batch, per, side, side), values.dtype),
        part=pltpu.VMEM((rows, wide, side), f32),
        in_code=pltpu.VMEM((2, rows, wide, side), jnp.int16),
        in_step=pltpu.VMEM((2, rows, 1, lanes), f32),
        out_code=pltpu.VMEM((2, rows, wide, side), jnp.int16),
        out_step=pltpu.VMEM((2, rows, 1, lanes), f32),
        sums=pltpu.VMEM((items + 1, wide, side), f32),
        mine=pltpu.VMEM((now, wide, side), f32),
        held_sem=pltpu.SemaphoreType.DMA((n,)),
        ring_sem=pltpu.SemaphoreType.DMA((slots,)),
        send_sem=pltpu.SemaphoreType.DMA((2, 2, pieces)),
        recv_sem=pltpu.SemaphoreType.DMA((2, 2, pieces)),
        mine_sem=pltpu.SemaphoreType.DMA((len(cuts),)),
    )

    def group(name, shapes):
        scratch.update({f"{name}{i}": shape for i, shape in enumerate(shapes)})
        return [f"{name}{i}" for i in range(len(shapes))]

    now_names = group("now", reduce_scratch(n, now, now_size, wide, side, lanes))
    if following is not None:
        args.update(following=following)
        specs.append(ANY)
        outs.update(
            following_slab=jax.ShapeDtypeStruct(slab.shape, slab.dtype),
            rest_out=jax.ShapeDtypeStruct((n * late, wide, side), f32),
        )
        early_names = group("early", gather_sems(n, half, gather_size))
        after_names = group("after", gather_sems(n, late, late_size))
        scratch.update(
            shelf=pltpu.VMEM((2, late_size, wide, side), f32),
            shelf_sem=pltpu.SemaphoreType.DMA((2,)),
        )
    if rest is not None:
        args.update(rest=rest)
        specs.append(ANY)
        outs.update(rest_piece=jax.ShapeDtypeStruct((late, wide, side), f32))
        late_names = group("late", reduce_scratch(n, late, late_size, wide, side, lanes))
        scratch.update(
            zs=pltpu.VMEM((n * late, wide, side), f32),
            zs_sem=pltpu.SemaphoreType.DMA(()),
        )
    names = list(args) + list(outs) + list(scratch)
    names[len(args) : len(args) + len(outs)] = [f"{name}_ref" for name in outs]
    names[: len(args)] = [f"{name}_ref" for name in args]

    def body(*refs):
        g = dict(zip(names, refs, strict=True))
        cols_ref, weights_ref, prev_ref, last_ref = (
            g[k] for k in ("cols_ref", "weights_ref", "prev_ref", "last_ref")
        )
        held, ring, part_ref, sums = g["held"], g["ring"], g["part"], g["sums"]
        in_code, in_step, out_code, out_step = (
            g[k] for k in ("in_code", "in_step", "out_code", "out_step")
        )
        me = lax.axis_index("blk")
        eye = diagonal(wide, lanes)

        def load(c):
            slot = c % slots
            return pltpu.make_async_copy(
                g["values_ref"].at[pl.ds(c * batch, batch)], ring.at[slot], g["ring_sem"].at[slot]
            )

        def shard(d, src):
            return pltpu.make_async_copy(
                src, held.at[pl.ds(d * blocks, blocks)], g["held_sem"].at[d]
            )

        load(0).start()
        for d in range(n):

            @pl.when(me == d)
            def _(d=d):
                shard(d, g["own_ref"]).start()

            @pl.when(me != d)
            def _(d=d):
                shard(d, g["slab_ref"].at[pl.ds(d * blocks, blocks)]).start()

        if rest is not None:
            zs_copy = pltpu.make_async_copy(g["rest_ref"], g["zs"], g["zs_sem"])
            zs_copy.start()
        greet(me, n)
        sums[items] = jnp.zeros((wide, side), f32)

        @pl.when(me == 0)
        def _():
            in_step[0] = jnp.zeros((rows, 1, lanes), f32)

        @pl.when(me == n - 1)
        def _():
            in_step[1] = jnp.zeros((rows, 1, lanes), f32)

        extra = []
        ends = []
        if following is not None:
            step, steps, finish = gather_steps(
                me, n, 0, half, gather_size, g["following_ref"], g["following_slab_ref"],
                *(g[k] for k in early_names),
            )
            extra.append((step, steps))
            ends.append(finish)
        if rest is not None:
            zs = g["zs"]

            def read_rest(d, c):
                return zs[pl.ds(d * late + c * late_size, late_size)]

            step, steps, finish = reduce_steps(
                me, n, late, late_size, eye, read_rest, zs, me * late,
                [g[k] for k in late_names], following is not None,
            )
            extra.append((step, steps))
            ends.append(finish)
            zs_copy.wait()

        for d in range(n):
            shard(d, g["own_ref"]).wait()

        def copies(way, c):
            to = {"blk": me + 1 - 2 * way}
            at = pl.ds(c * batch, batch)
            return [
                pltpu.make_async_remote_copy(
                    src_ref=src.at[way, at],
                    dst_ref=dst.at[way, at],
                    send_sem=g["send_sem"].at[way, kind, c],
                    recv_sem=g["recv_sem"].at[way, kind, c],
                    device_id=to,
                    device_id_type=MESH,
                )
                for kind, (src, dst) in enumerate(((out_code, in_code), (out_step, in_step)))
            ]

        def incoming(way, c):
            at = pl.ds(c * batch, batch)
            return decode(in_code[way, at], in_step[way, at], eye)

        def relay(way, c, has, goes):
            @pl.when((c >= 0) & (c < pieces) & has)
            def _():
                for one in copies(way, c):
                    one.wait_recv()

            @pl.when((c >= 0) & (c < pieces) & goes)
            def _():
                at = pl.ds(c * batch, batch)
                code, step = encode(part_ref[at] + incoming(way, c), eye)
                out_code[way, at] = code
                out_step[way, at] = step
                for one in copies(way, c):
                    one.start()

        first_steps = max([pieces + lag] + [steps for _, steps in extra])

        @pl.loop(0, first_steps)
        def _(s):
            @pl.when(s + 1 < pieces)
            def _():
                load(s + 1).start()

            @pl.when(s < pieces)
            def _():
                load(s).wait()
                for r in range(batch):
                    total = None
                    for k in range(per):
                        at = (s * batch + r) * per + k
                        term = weights_ref[at] * lax.dot_general(
                            held[cols_ref[at]],
                            ring[s % slots, r, k],
                            (((1,), (1,)), ((), ())),
                            preferred_element_type=f32,
                        )
                        total = term if total is None else total + term
                    part_ref[s * batch + r] = total

            relay(0, s - HOP * me, me > 0, me < n - 1)
            relay(1, s - HOP * (n - 1 - me), me < n - 1, me > 0)
            for step, steps in extra:

                @pl.when(s < steps)
                def _(step=step):
                    step(s)

            c = s - lag

            @pl.when((c >= 0) & (c < pieces))
            def _():
                total = part_ref[pl.ds(c * batch, batch)] + incoming(0, c) + incoming(1, c)
                high = total.astype(jnp.bfloat16)
                low = (total - high.astype(f32)).astype(jnp.bfloat16)
                for r in range(batch):
                    both = jnp.concatenate([high[r], low[r]], axis=0)
                    for k in range(per):
                        at = (c * batch + r) * per + k
                        pair = lax.dot_general(
                            both,
                            ring[c % slots, r, k],
                            (((1,), (0,)), ((), ())),
                            preferred_element_type=f32,
                        )
                        term = weights_ref[at] * (pair[:wide] + pair[wide:])
                        sums[at] = term + sums[prev_ref[at]]

        if rest is not None:
            rest_copy = pltpu.make_async_copy(
                g["zs"].at[pl.ds(me * late, late)], g["rest_piece_ref"], g["zs_sem"]
            )
            rest_copy.start()

        mine = g["mine"]

        @pl.loop(0, now)
        def _(i):
            mine[i] = sums[last_ref[me * blocks + i]]

        def read_now(d, c):
            first = d * blocks + c * now_size
            return jnp.stack([sums[last_ref[first + i]] for i in range(now_size)])

        step, steps, finish = reduce_steps(
            me, n, now, now_size, eye, read_now, mine, 0, [g[k] for k in now_names],
            following is not None,
        )
        second = [(step, steps)]
        ends.append(finish)
        if following is not None:
            step, steps, finish = gather_steps(
                me, n, half, late, late_size, g["following_ref"], g["following_slab_ref"],
                *(g[k] for k in after_names),
            )
            second.append((step, steps))
            ends.append(finish)
            shelf = g["shelf"]
            shelves = n * late // late_size
            per_shard = late // late_size

            def store(i):
                return pltpu.make_async_copy(
                    shelf.at[i % 2],
                    g["rest_out_ref"].at[pl.ds(i * late_size, late_size)],
                    g["shelf_sem"].at[i % 2],
                )

            def keep(i):
                @pl.when(i >= 2)
                def _():
                    store(i - 2).wait()

                first = i // per_shard * blocks + half + i % per_shard * late_size
                for j in range(late_size):
                    shelf[i % 2, j] = sums[last_ref[first + j]]
                store(i).start()

            second.append((keep, shelves))

        @pl.loop(0, max(steps for _, steps in second))
        def _(s):
            for step, steps in second:

                @pl.when(s < steps)
                def _(step=step):
                    step(s)

        mine_copies = [
            pltpu.make_async_copy(
                mine.at[pl.ds(a, b - a)], g[f"piece{i}_ref"], g["mine_sem"].at[i]
            )
            for i, (a, b) in enumerate(cuts)
        ]
        for one in mine_copies:
            one.start()

        @pl.loop(0, pieces)
        def _(c):
            @pl.when(me < n - 1)
            def _():
                for one in copies(0, c):
                    one.wait_send()

            @pl.when(me > 0)
            def _():
                for one in copies(1, c):
                    one.wait_send()

        for finish in ends:
            finish()
        if following is not None:
            for i in range(max(shelves - 2, 0), shelves):
                store(i).wait()
        if rest is not None:
            rest_copy.wait()
        for one in mine_copies:
            one.wait()

    results = pl.pallas_call(
        body,
        out_shape=list(outs.values()),
        in_specs=specs,
        out_specs=[ANY] * len(outs),
        scratch_shapes=list(scratch.values()),
        compiler_params=pltpu.CompilerParams(
            collective_id=2 + part, has_side_effects=True, vmem_limit_bytes=63 << 20
        ),
        name=f"stage_{part}",
    )(*args.values())
    return dict(zip(outs, results))


def all_sum(x, axis):
    n = lax.axis_size(axis)
    if n & (n - 1):
        return lax.psum(x, axis)
    bit = 1
    while bit < n:
        x = x + lax.ppermute(x, axis, [(i, i ^ bit) for i in range(n)])
        bit *= 2
    return x


def join(z_refs, early, b):
    here = [z_refs[2 * p + (0 if early else 1)][b] for p in range(len(z_refs) // 2)]
    return jnp.concatenate(here, axis=0)


def block_specs(pieces, batch, early_steps):
    specs = []
    for i, piece in enumerate(pieces):
        shape = (batch,) + piece.shape[1:]
        if i % 2 == 0:
            specs.append(pl.BlockSpec(shape, lambda i: (jnp.minimum(i, early_steps - 1), 0, 0)))
        else:
            specs.append(pl.BlockSpec(shape, lambda i: (jnp.maximum(i - early_steps, 0), 0, 0)))
    return specs


def halves(x):
    high = x.astype(jnp.bfloat16)
    return high, (x - high.astype(jnp.float32)).astype(jnp.bfloat16)


def outer(x, y):
    return lax.dot_general(x, y, (((1,), (1,)), ((), ())), preferred_element_type=jnp.float32)


def gram_of(pieces):
    early, late = pieces[0].shape[0], pieces[1].shape[0]
    side = pieces[0].shape[2]
    width = sum(piece.shape[1] for piece in pieces[::2])
    batch = divisor(math.gcd(early, late), 8)

    def body(*refs):
        *z_refs, out_ref, main, cross = refs

        @pl.when(pl.program_id(0) == 0)
        def _():
            main[...] = jnp.zeros_like(main)
            cross[...] = jnp.zeros_like(cross)

        for first in (True, False):

            @pl.when((pl.program_id(0) < early // batch) == first)
            def _(first=first):
                for b in range(batch):
                    high, low = halves(join(z_refs, first, b))
                    main[...] += outer(high, high)
                    cross[...] += outer(high, low)

        @pl.when(pl.program_id(0) == pl.num_programs(0) - 1)
        def _():
            out_ref[...] = main[...] + (cross[...] + cross[...].T)

    return pl.pallas_call(
        body,
        out_shape=jax.ShapeDtypeStruct((width, width), jnp.float32),
        grid=((early + late) // batch,),
        in_specs=block_specs(pieces, batch, early // batch),
        out_specs=pl.BlockSpec((width, width), lambda i: (0, 0)),
        scratch_shapes=[pltpu.VMEM((width, width), jnp.float32)] * 2,
        name="gram",
    )(*pieces)


def crossed(x, y):
    return lax.dot_general(x, y, (((0,), (1,)), ((), ())), preferred_element_type=jnp.float32)


def solve(pieces, inverse):
    early, late = pieces[0].shape[0], pieces[1].shape[0]
    side = pieces[0].shape[2]
    width = sum(piece.shape[1] for piece in pieces[::2])
    batch = divisor(math.gcd(early, late), 8)

    def body(*refs):
        *z_refs, inverse_ref, out_ref = refs
        inv_high, inv_low = halves(inverse_ref[...])
        inv_twice = jnp.concatenate([inv_high, inv_high], axis=1)
        for first in (True, False):

            @pl.when((pl.program_id(0) < early // batch) == first)
            def _(first=first):
                for b in range(batch):
                    high, low = halves(join(z_refs, first, b))
                    both = jnp.concatenate([high, low], axis=0)
                    out_ref[b] = crossed(both, inv_twice) + crossed(high, inv_low)

    return pl.pallas_call(
        body,
        out_shape=jax.ShapeDtypeStruct((early + late, side, width), jnp.float32),
        grid=((early + late) // batch,),
        in_specs=block_specs(pieces, batch, early // batch)
        + [pl.BlockSpec((width, width), lambda i: (0, 0))],
        out_specs=pl.BlockSpec((batch, side, width), lambda i: (i, 0, 0)),
        name="solve",
    )(*pieces, inverse)


def local(values, scales, pattern, omega):
    rows, per = pattern.shape
    blocks, side, width = omega.shape
    n = lax.axis_size("blk")
    items = rows * per
    columns = blocks * n
    cols = pattern.reshape(-1) - lax.axis_index("row") * columns
    weights = scales.astype(jnp.float32).reshape(-1)
    slot = jnp.arange(items)
    same = cols[:, None] == cols[None, :]
    prev = jnp.max(jnp.where(same & (slot[None, :] < slot[:, None]), slot[None, :], -1), axis=1)
    prev = jnp.where(prev < 0, items, prev)
    hits = jnp.arange(columns)[:, None] == cols[None, :]
    last = jnp.max(jnp.where(hits, slot[None, :], -1), axis=1)
    last = jnp.where(last < 0, items, last)

    parts = 4
    wide = width // parts
    turned = jnp.transpose(omega, (0, 2, 1)).reshape(blocks, parts, wide, side)
    own = [turned[:, p] for p in range(parts)]
    slab = gather(own[0], n)
    rest = None
    pieces = []
    for p in range(parts):
        following = own[p + 1] if p + 1 < parts else None
        done = stage(p, values, own[p], slab, (cols, weights, prev, last), n, following, rest)
        if p:
            pieces.append(done["rest_piece"])
        if p + 1 < parts:
            pieces.append(done["piece0"])
            slab, rest = done["following_slab"], done["rest_out"]
        else:
            pieces += [done["piece0"], done["piece1"]]

    total_rows = columns * side * lax.axis_size("row")
    gram = all_sum(all_sum(gram_of(pieces), "row"), "blk") / total_rows
    lower = jnp.linalg.cholesky(gram)
    inverse = jax.scipy.linalg.solve_triangular(lower, jnp.eye(width, dtype=jnp.float32), lower=True)
    return solve(pieces, inverse), lower.T


def solution(mesh):
    return jax.shard_map(
        local,
        mesh=mesh,
        in_specs=(
            P("row", "blk", None, None),
            P("row", "blk"),
            P("row", "blk"),
            P(("row", "blk"), None, None),
        ),
        out_specs=(P(("row", "blk"), None, None), P()),
        check_vma=False,
    )
```

time: 748 us -> 672 us (0.90)
  Pallas kernels: 677 us -> 609 us
  other arithmetic: 32.1 us -> 24.4 us
    pallas_call x1, Pallas kernels: 141 us -> 75.1 us  [gather(): pl.pallas_call(body, out_shape=jax.ShapeDtypeStruct((n * blocks,) + own.s...]
    concatenate x1 -> x0, other arithmetic: 7.69 us -> none  [local(): flat = jnp.concatenate(sums, axis=1)]
where the time goes in v1:
time: 672 us; the launch traced here: 670 us
  Pallas kernels  609 us (91%)
  other arithmetic  24.4 us (4%)
  local copies, waits for them, and re-layouts  14 us (2%)
  waiting for transfers between devices  13.8 us (2%)
  starting transfers between devices  7.74 us (1%)
    pallas_call x4, Pallas kernels, stage(): pl.pallas_call(body, out_shape=list(outs.values()), in_specs=specs, out_s...  515 us
    pallas_call x1, Pallas kernels, gather(): pl.pallas_call(body, out_shape=jax.ShapeDtypeStruct((n * blocks,) + own.s...  75.1 us
    ppermute x5, waiting for transfers between devices, all_sum(): x = x + lax.ppermute(x, axis, [(i, i ^ bit) for i in range(n)])  13.8 us
  transfers between devices with their start and end apart: 5, of which 5 were waited for; matrix products, arithmetic and copies ran while one was open for 0% of the time, Pallas kernels for 0%

profile of v1, /device:TPU:0, one launch (start us, length us, event | category | flops | bytes accessed | tf_op | source)
XLA Modules:
  0.0 670.4 jit_solution(16555238483800525400)
XLA Ops:
  0.6 0.7 broadcast_subtract_fusion
  1.3 0.1 copy.21
  1.4 0.1 sub.10.refs_0_
  1.5 0.2 select_reduce_fusion
  1.7 0.8 copy.22
  2.5 0.7 reshape.39.refs_1_
  3.2 6.4 copy.23
  9.6 4.2 slice_bitcast_fusion
  13.8 75.1 %gather.1.refs_6_ = bf16[256,32,256]{2,1,0:T(8,128)(2,1)} custom-call(bf16[64,32,256]{2,1,0:T(8,128)(2,1)} %get-tuple-element.41.own_ref.refs_5_), custom_call_target="tpu_custom_call" | custom-call | tf_op jit(solution)/shard_map/gather/pallas_call | solution.py:137
  88.9 0.6 compare_select_fusion
  89.5 117.7 %stage_0.1 = (f32[32,32,256]{2,1,0:T(8,128)}, bf16[256,32,256]{2,1,0:T(8,128)(2,1)}, f32[128,32,256]{2,1,0:T(8,128)}) custom-call(s32[256]{0:T(256)} %copy-done, f32[256]{0:T(256)} %reshape.39.refs_1_, s32[256]{0:T(256)} %get-tuple-element.45.refs_2_, s32[256]{0:T(256)} %get-tuple-element.44.refs_3_, bf16[64,4,256,256]{3,2,1,0:T(8,128)(2,1)} %refs_4_.7, ...), custom_call_target="tpu_custom_call" | custom-call | tf_op jit(solution)/shard_map/stage_0/pallas_call | solution.py:555
  207.2 132.2 %stage_1.1 = (f32[32,32,256]{2,1,0:T(8,128)}, bf16[256,32,256]{2,1,0:T(8,128)(2,1)}, f32[128,32,256]{2,1,0:T(8,128)}, f32[32,32,256]{2,1,0:T(8,128)}) custom-call(s32[256]{0:T(256)} %copy-done, f32[256]{0:T(256)} %reshape.39.refs_1_, s32[256]{0:T(256)} %get-tuple-element.45.refs_2_, s32[256]{0:T(256)} %get-tuple-element.44.refs_3_, ...), custom_call_target="tpu_custom_call" | custom-call | tf_op jit(solution)/shard_map/stage_1/pallas_call | solution.py:555
  339.4 130.8 %stage_2.1 = (f32[32,32,256]{2,1,0:T(8,128)}, bf16[256,32,256]{2,1,0:T(8,128)(2,1)}, f32[128,32,256]{2,1,0:T(8,128)}, f32[32,32,256]{2,1,0:T(8,128)}) custom-call(s32[256]{0:T(256)} %copy-done, f32[256]{0:T(256)} %reshape.39.refs_1_, s32[256]{0:T(256)} %get-tuple-element.45.refs_2_, s32[256]{0:T(256)} %get-tuple-element.44.refs_3_, ...), custom_call_target="tpu_custom_call" | custom-call | tf_op jit(solution)/shard_map/stage_2/pallas_call | solution.py:555
  470.2 134.2 %stage_3.1 = (f32[32,32,256]{2,1,0:T(8,128)}, f32[32,32,256]{2,1,0:T(8,128)}, f32[32,32,256]{2,1,0:T(8,128)}) custom-call(s32[256]{0:T(256)} %copy-done, f32[256]{0:T(256)} %reshape.39.refs_1_, s32[256]{0:T(256)} %get-tuple-element.45.refs_2_, s32[256]{0:T(256)} %get-tuple-element.44.refs_3_, bf16[64,4,256,256]{3,2,1,0:T(8,128)(2,1)} %refs_4_.7, ...), custom_call_target="tpu_custom_call" | custom-call | tf_op jit(solution)/shard_map/stage_3/pallas_call | solution.py:555
  604.4 8.3 %gram.1 = f32[128,128]{1,0:T(8,128)} custom-call(f32[32,32,256]{2,1,0:T(8,128)} %get-tuple-element.16.refs_0_, f32[32,32,256]{2,1,0:T(8,128)} %get-tuple-element.19.refs_1_, f32[32,32,256]{2,1,0:T(8,128)} %get-tuple-element.20.refs_2_, f32[32,32,256]{2,1,0:T(8,128)} %get-tuple-element.23.refs_3_, f32[32,32,256]{2,1,0:T(8,128)} %get-tuple-element.24.refs_4_, ...), custom_call_target="tpu_custom_call" | custom-call | tf_op jit(solution)/shard_map/gram/pallas_call | solution.py:632
  612.7 0.9 copy.29
  613.7 1.2 collective-permute-done
  615.0 1.5 collective-permute-start.1
  616.5 2.8 collective-permute-done.1
  619.3 1.6 collective-permute-start.2
  620.9 2.7 collective-permute-done.2
  623.7 4.1 collective-permute-start.3
  627.8 2.2 collective-permute-done.3
  630.1 0.5 collective-permute-start.4
  630.5 4.8 collective-permute-done.4
  635.4 11.7 %cholesky.17 = f32[128,128]{1,0:T(8,128)S(1)} custom-call(f32[128,128]{1,0:T(8,128)S(1)} %fusion.3), custom_call_target="Cholesky" | custom-call | tf_op jit(solution)/shard_map/jit(cholesky)/cholesky | solution.py:713
  647.2 0.6 compare_reduce_fusion
  647.8 0.7 fusion.4
  648.5 0.7 copy.31
  649.2 9.8 %custom-call.7 = f32[1,128,128]{1,2,0:T(8,128)S(1)} custom-call(f32[1,128,128]{2,1,0:T(8,128)S(1)} %get-tuple-element.43), custom_call_target="InvertDiagBlocksLowerTriangular" | custom-call | tf_op jit(solution)/shard_map/jit(_solve_triangular)/triangular_solve | solution.py:714
  659.0 0.9 fusion.1.refs_8_
  659.9 10.5 %solve.1 = f32[64,256,128]{2,1,0:T(8,128)} custom-call(f32[32,32,256]{2,1,0:T(8,128)} %get-tuple-element.16.refs_0_, f32[32,32,256]{2,1,0:T(8,128)} %get-tuple-element.19.refs_1_, f32[32,32,256]{2,1,0:T(8,128)} %get-tuple-element.20.refs_2_, f32[32,32,256]{2,1,0:T(8,128)} %get-tuple-element.23.refs_3_, f32[32,32,256]{2,1,0:T(8,128)} %get-tuple-element.24.refs_4_, ...), custom_call_target="tpu_custom_call" | custom-call | tf_op jit(solution)/shard_map/solve/pallas_call | solution.py:666
  (11 shorter events, 0.3 us)
Async XLA Ops:
  1.5 8.0 %copy-start = (s32[256]{0:T(256)}, s32[256]{0:T(256)S(1)}, u32[]{:S(2)}) copy-start(s32[256]{0:T(256)S(1)} %sub.10.refs_0_) | copy-start | bytes 3076
  613.7 1.3 collective-permute-start
  615.0 4.3 collective-permute-start.1
  619.3 4.3 collective-permute-start.2
  623.7 6.4 collective-permute-start.3
  630.1 5.2 collective-permute-start.4

commit v2 on v1

--- a/solution.py
+++ b/solution.py
@@ -25,7 +25,7 @@
 
 
 def encode(x, eye):
-    peak = jnp.max(jnp.abs(x), axis=2, keepdims=True)
+    peak = jnp.max(jnp.max(jnp.abs(x), axis=0, keepdims=True), axis=2, keepdims=True)
     live = peak > TINY
     inverse = jnp.where(live, LEVELS / jnp.where(live, peak, 1.0), 0.0)
     code = jnp.round(x * inverse).astype(jnp.int32).astype(jnp.int16)
@@ -123,47 +123,90 @@
     return [pltpu.SemaphoreType.DMA((2, n - 1, count // size))] * 2
 
 
-def gather(own, n):
-    blocks = own.shape[0]
+def gather(omega, n, parts):
+    blocks, side, width = omega.shape
+    wide = width // parts
     size = divisor(blocks, 4)
-
-    def body(own_ref, slab_ref, *sems):
+    pieces = blocks // size
+
+    def body(omega_ref, *refs):
+        slab_ref, *own_refs = refs[: 1 + parts]
+        raw, turned, raw_sem, own_sem, *sems = refs[1 + parts :]
         me = lax.axis_index("blk")
+
+        def load(c):
+            at = pl.ds(c * size, size)
+            return pltpu.make_async_copy(omega_ref.at[at], raw.at[at], raw_sem.at[c])
+
+        def keep(p, c):
+            at = pl.ds(c * size, size)
+            return pltpu.make_async_copy(turned.at[p, at], own_refs[p].at[at], own_sem.at[p, c])
+
+        for c in range(pieces):
+            load(c).start()
         greet(me, n)
-        step, steps, finish = gather_steps(me, n, 0, blocks, size, own_ref, slab_ref, *sems)
-        pl.loop(0, steps)(step)
+        step, steps, finish = gather_steps(me, n, 0, blocks, size, turned.at[0], slab_ref, *sems)
+
+        @pl.loop(0, steps)
+        def _(s):
+            @pl.when(s < pieces)
+            def _():
+                load(s).wait()
+                for i in range(size):
+                    block = raw[s * size + i].T
+                    for p in range(parts):
+                        turned[p, s * size + i] = block[p * wide : (p + 1) * wide]
+
+            step(s)
+
+            @pl.when(s < pieces)
+            def _():
+                for p in range(parts):
+                    keep(p, s).start()
+
         finish()
+
+        @pl.loop(0, pieces)
+        def _(c):
+            for p in range(parts):
+                keep(p, c).wait()
 
     return pl.pallas_call(
         body,
-        out_shape=jax.ShapeDtypeStruct((n * blocks,) + own.shape[1:], own.dtype),
+        out_shape=[jax.ShapeDtypeStruct((n * blocks, wide, side), omega.dtype)]
+        + [jax.ShapeDtypeStruct((blocks, wide, side), omega.dtype)] * parts,
         in_specs=[ANY],
-        out_specs=ANY,
-        scratch_shapes=gather_sems(n, blocks, size),
+        out_specs=[ANY] * (1 + parts),
+        scratch_shapes=[
+            pltpu.VMEM(omega.shape, omega.dtype),
+            pltpu.VMEM((parts, blocks, wide, side), omega.dtype),
+            pltpu.SemaphoreType.DMA((pieces,)),
+            pltpu.SemaphoreType.DMA((parts, pieces)),
+        ]
+        + gather_sems(n, blocks, size),
         compiler_params=pltpu.CompilerParams(collective_id=1, has_side_effects=True),
         name="gather",
-    )(own)
+    )(omega)
 
 
 def reduce_scratch(n, count, size, wide, side, lanes):
     far = (n - 1) * count
     sems = pltpu.SemaphoreType.DMA((2, 2, far // size))
     code = pltpu.VMEM((2, far, wide, side), jnp.int16)
-    step = pltpu.VMEM((2, far, 1, lanes), jnp.float32)
+    step = pltpu.VMEM((2, far // size, 1, lanes), jnp.float32)
     return [code, step, code, step, sems, sems]
 
 
-def reduce_steps(me, n, count, size, eye, read, total, base, scratch, beside):
+def reduce_steps(me, n, count, size, eye, read, total, base, scratch, beside, start):
     in_code, in_step, out_code, out_step, send_sem, recv_sem = scratch
     pieces = count // size
     reach = (n - 1) * pieces
     far = ((n - 1 - me) * pieces, me * pieces)
     hop = max(pieces, HOP) if beside else HOP
-    start = pieces if beside else 0
 
     def copies(way, u):
-        here = pl.ds(u * size, size)
         to = {"blk": me + 1 - 2 * way}
+        pairs = (out_code, in_code, pl.ds(u * size, size)), (out_step, in_step, pl.ds(u, 1))
         return [
             pltpu.make_async_remote_copy(
                 src_ref=src.at[way, here],
@@ -173,18 +216,16 @@
                 device_id=to,
                 device_id_type=MESH,
             )
-            for kind, (src, dst) in enumerate(((out_code, in_code), (out_step, in_step)))
+            for kind, (src, dst, here) in enumerate(pairs)
         ]
 
     def incoming(way, u):
-        here = pl.ds(u * size, size)
-        return decode(in_code[way, here], in_step[way, here], eye)
+        return decode(in_code[way, pl.ds(u * size, size)], in_step[way, pl.ds(u, 1)], eye)
 
     def push(way, u, value):
-        here = pl.ds(u * size, size)
         code, step = encode(value, eye)
-        out_code[way, here] = code
-        out_step[way, here] = step
+        out_code[way, pl.ds(u * size, size)] = code
+        out_step[way, pl.ds(u, 1)] = step
         for one in copies(way, u):
             one.start()
 
@@ -258,9 +299,9 @@
         ring=pltpu.VMEM((slots, batch, per, side, side), values.dtype),
         part=pltpu.VMEM((rows, wide, side), f32),
         in_code=pltpu.VMEM((2, rows, wide, side), jnp.int16),
-        in_step=pltpu.VMEM((2, rows, 1, lanes), f32),
+        in_step=pltpu.VMEM((2, pieces, 1, lanes), f32),
         out_code=pltpu.VMEM((2, rows, wide, side), jnp.int16),
-        out_step=pltpu.VMEM((2, rows, 1, lanes), f32),
+        out_step=pltpu.VMEM((2, pieces, 1, lanes), f32),
         sums=pltpu.VMEM((items + 1, wide, side), f32),
         mine=pltpu.VMEM((now, wide, side), f32),
         held_sem=pltpu.SemaphoreType.DMA((n,)),
@@ -343,11 +384,11 @@
 
         @pl.when(me == 0)
         def _():
-            in_step[0] = jnp.zeros((rows, 1, lanes), f32)
+            in_step[0] = jnp.zeros((pieces, 1, lanes), f32)
 
         @pl.when(me == n - 1)
         def _():
-            in_step[1] = jnp.zeros((rows, 1, lanes), f32)
+            in_step[1] = jnp.zeros((pieces, 1, lanes), f32)
 
         extra = []
         ends = []
@@ -356,8 +397,11 @@
                 me, n, 0, half, gather_size, g["following_ref"], g["following_slab_ref"],
                 *(g[k] for k in early_names),
             )
-            extra.append((step, steps))
+            lead = min(2, steps)
+            extra.append((lambda s, step=step: step(s + lead), steps - lead))
             ends.append(finish)
+            for v in range(lead):
+                step(v)
         if rest is not None:
             zs = g["zs"]
 
@@ -367,6 +411,7 @@
             step, steps, finish = reduce_steps(
                 me, n, late, late_size, eye, read_rest, zs, me * late,
                 [g[k] for k in late_names], following is not None,
+                max(half // gather_size - 2, 0) if following is not None else 0,
             )
             extra.append((step, steps))
             ends.append(finish)
@@ -377,22 +422,25 @@
 
         def copies(way, c):
             to = {"blk": me + 1 - 2 * way}
-            at = pl.ds(c * batch, batch)
+            pairs = (
+                (out_code, in_code, pl.ds(c * batch, batch)),
+                (out_step, in_step, pl.ds(c, 1)),
+            )
             return [
                 pltpu.make_async_remote_copy(
-                    src_ref=src.at[way, at],
-                    dst_ref=dst.at[way, at],
+                    src_ref=src.at[way, here],
+                    dst_ref=dst.at[way, here],
                     send_sem=g["send_sem"].at[way, kind, c],
                     recv_sem=g["recv_sem"].at[way, kind, c],
                     device_id=to,
                     device_id_type=MESH,
                 )
-                for kind, (src, dst) in enumerate(((out_code, in_code), (out_step, in_step)))
+                for kind, (src, dst, here) in enumerate(pairs)
             ]
 
         def incoming(way, c):
-            at = pl.ds(c * batch, batch)
-            return decode(in_code[way, at], in_step[way, at], eye)
+            code = in_code[way, pl.ds(c * batch, batch)]
+            return decode(code, in_step[way, pl.ds(c, 1)], eye)
 
         def relay(way, c, has, goes):
             @pl.when((c >= 0) & (c < pieces) & has)
@@ -405,11 +453,18 @@
                 at = pl.ds(c * batch, batch)
                 code, step = encode(part_ref[at] + incoming(way, c), eye)
                 out_code[way, at] = code
-                out_step[way, at] = step
+                out_step[way, pl.ds(c, 1)] = step
                 for one in copies(way, c):
                     one.start()
 
         first_steps = max([pieces + lag] + [steps for _, steps in extra])
+        if following is not None:
+            late_step, late_steps, finish = gather_steps(
+                me, n, half, late, late_size, g["following_ref"], g["following_slab_ref"],
+                *(g[k] for k in after_names),
+            )
+            ends.append(finish)
+            ahead = late // late_size
 
         @pl.loop(0, first_steps)
         def _(s):
@@ -440,6 +495,12 @@
                 @pl.when(s < steps)
                 def _(step=step):
                     step(s)
+
+            if following is not None:
+
+                @pl.when(s >= first_steps - ahead)
+                def _():
+                    late_step(s - (first_steps - ahead))
 
             c = s - lag
 
@@ -479,17 +540,12 @@
 
         step, steps, finish = reduce_steps(
             me, n, now, now_size, eye, read_now, mine, 0, [g[k] for k in now_names],
-            following is not None,
+            following is not None, 0,
         )
         second = [(step, steps)]
         ends.append(finish)
         if following is not None:
-            step, steps, finish = gather_steps(
-                me, n, half, late, late_size, g["following_ref"], g["following_slab_ref"],
-                *(g[k] for k in after_names),
-            )
-            second.append((step, steps))
-            ends.append(finish)
+            second.append((lambda s: late_step(s + ahead), late_steps - ahead))
             shelf = g["shelf"]
             shelves = n * late // late_size
             per_shard = late // late_size
@@ -691,10 +747,7 @@
     last = jnp.where(last < 0, items, last)
 
     parts = 4
-    wide = width // parts
-    turned = jnp.transpose(omega, (0, 2, 1)).reshape(blocks, parts, wide, side)
-    own = [turned[:, p] for p in range(parts)]
-    slab = gather(own[0], n)
+    slab, *own = gather(omega, n, parts)
     rest = None
     pieces = []
     for p in range(parts):

time: 672 us -> 647 us (0.963)
  Pallas kernels: 609 us -> 595 us
  local copies, waits for them, and re-layouts: 14 us -> 3.4 us
    pallas_call x4, Pallas kernels: 515 us -> 500 us  [stage(): pl.pallas_call(body, out_shape=list(outs.values()), in_specs=specs, out_s...]
where the time goes in v2:
time: 647 us; the launch traced here: 646 us
  Pallas kernels  595 us (92%)
  other arithmetic  24.4 us (4%)
  waiting for transfers between devices  13 us (2%)
  starting transfers between devices  8.5 us (1%)
    pallas_call x4, Pallas kernels, stage(): pl.pallas_call(body, out_shape=list(outs.values()), in_specs=specs, out_s...  500 us
    pallas_call x1, Pallas kernels, gather(): pl.pallas_call(body, out_shape=[jax.ShapeDtypeStruct((n * blocks, wide, s...  76 us
    ppermute x5, waiting for transfers between devices, all_sum(): x = x + lax.ppermute(x, axis, [(i, i ^ bit) for i in range(n)])  13 us
  transfers between devices with their start and end apart: 5, of which 5 were waited for; matrix products, arithmetic and copies ran while one was open for 0% of the time, Pallas kernels for 0%

profile of v2, /device:TPU:0, one launch (start us, length us, event | category | flops | bytes accessed | tf_op | source)
XLA Modules:
  0.0 645.6 jit_solution(4757989494128894759)
XLA Ops:
  0.6 0.7 broadcast_subtract_fusion
  1.3 0.1 copy.16
  1.4 0.1 sub.10.refs_0_
  1.5 0.2 select_reduce_fusion
  1.7 0.8 copy.17
  2.5 0.7 reshape.35.refs_1_
  3.2 76.0 %gather.1 = (bf16[256,32,256]{2,1,0:T(8,128)(2,1)}, bf16[64,32,256]{2,1,0:T(8,128)(2,1)}, bf16[64,32,256]{2,1,0:T(8,128)(2,1)}, bf16[64,32,256]{2,1,0:T(8,128)(2,1)}, bf16[64,32,256]{2,1,0:T(8,128)(2,1)}) custom-call(bf16[64,256,128]{2,1,0:T(8,128)(2,1)} %omega_ref.1), custom_call_target="tpu_custom_call" | custom-call | tf_op jit(solution)/shard_map/gather/pallas_call | solution.py:174
  79.2 0.6 compare_select_fusion
  79.7 114.1 %stage_0.1 = (f32[32,32,256]{2,1,0:T(8,128)}, bf16[256,32,256]{2,1,0:T(8,128)(2,1)}, f32[128,32,256]{2,1,0:T(8,128)}) custom-call(s32[256]{0:T(256)} %copy-done, f32[256]{0:T(256)} %reshape.35.refs_1_, s32[256]{0:T(256)} %get-tuple-element.51.refs_2_, s32[256]{0:T(256)} %get-tuple-element.50.refs_3_, bf16[64,4,256,256]{3,2,1,0:T(8,128)(2,1)} %refs_4_.7, ...), custom_call_target="tpu_custom_call" | custom-call | tf_op jit(solution)/shard_map/stage_0/pallas_call | solution.py:611
  193.8 127.8 %stage_1.1 = (f32[32,32,256]{2,1,0:T(8,128)}, bf16[256,32,256]{2,1,0:T(8,128)(2,1)}, f32[128,32,256]{2,1,0:T(8,128)}, f32[32,32,256]{2,1,0:T(8,128)}) custom-call(s32[256]{0:T(256)} %copy-done, f32[256]{0:T(256)} %reshape.35.refs_1_, s32[256]{0:T(256)} %get-tuple-element.51.refs_2_, s32[256]{0:T(256)} %get-tuple-element.50.refs_3_, ...), custom_call_target="tpu_custom_call" | custom-call | tf_op jit(solution)/shard_map/stage_1/pallas_call | solution.py:611
  321.6 127.0 %stage_2.1 = (f32[32,32,256]{2,1,0:T(8,128)}, bf16[256,32,256]{2,1,0:T(8,128)(2,1)}, f32[128,32,256]{2,1,0:T(8,128)}, f32[32,32,256]{2,1,0:T(8,128)}) custom-call(s32[256]{0:T(256)} %copy-done, f32[256]{0:T(256)} %reshape.35.refs_1_, s32[256]{0:T(256)} %get-tuple-element.51.refs_2_, s32[256]{0:T(256)} %get-tuple-element.50.refs_3_, ...), custom_call_target="tpu_custom_call" | custom-call | tf_op jit(solution)/shard_map/stage_2/pallas_call | solution.py:611
  448.6 131.1 %stage_3.1 = (f32[32,32,256]{2,1,0:T(8,128)}, f32[32,32,256]{2,1,0:T(8,128)}, f32[32,32,256]{2,1,0:T(8,128)}) custom-call(s32[256]{0:T(256)} %copy-done, f32[256]{0:T(256)} %reshape.35.refs_1_, s32[256]{0:T(256)} %get-tuple-element.51.refs_2_, s32[256]{0:T(256)} %get-tuple-element.50.refs_3_, bf16[64,4,256,256]{3,2,1,0:T(8,128)(2,1)} %refs_4_.7, ...), custom_call_target="tpu_custom_call" | custom-call | tf_op jit(solution)/shard_map/stage_3/pallas_call | solution.py:611
  579.8 8.3 %gram.1 = f32[128,128]{1,0:T(8,128)} custom-call(f32[32,32,256]{2,1,0:T(8,128)} %get-tuple-element.24.refs_0_, f32[32,32,256]{2,1,0:T(8,128)} %get-tuple-element.28.refs_1_, f32[32,32,256]{2,1,0:T(8,128)} %get-tuple-element.29.refs_2_, f32[32,32,256]{2,1,0:T(8,128)} %get-tuple-element.33.refs_3_, f32[32,32,256]{2,1,0:T(8,128)} %get-tuple-element.34.refs_4_, ...), custom_call_target="tpu_custom_call" | custom-call | tf_op jit(solution)/shard_map/gram/pallas_call | solution.py:688
  588.1 0.9 copy.19
  589.0 0.1 collective-permute-start
  589.1 1.2 collective-permute-done
  590.3 1.6 collective-permute-start.1
  591.9 2.7 collective-permute-done.1
  594.7 1.6 collective-permute-start.2
  596.3 2.7 collective-permute-done.2
  599.0 4.0 collective-permute-start.3
  603.1 2.2 collective-permute-done.3
  605.3 1.2 collective-permute-start.4
  606.5 4.0 collective-permute-done.4
  610.6 0.1 copy.20
  610.7 11.7 %cholesky.17 = f32[128,128]{1,0:T(8,128)S(1)} custom-call(f32[128,128]{1,0:T(8,128)S(1)} %fusion.3), custom_call_target="Cholesky" | custom-call | tf_op jit(solution)/shard_map/jit(cholesky)/cholesky | solution.py:766
  622.4 0.6 compare_reduce_fusion
  623.1 0.7 fusion.4
  623.7 0.7 copy.21
  624.5 9.8 %custom-call.7 = f32[1,128,128]{1,2,0:T(8,128)S(1)} custom-call(f32[1,128,128]{2,1,0:T(8,128)S(1)} %get-tuple-element.49), custom_call_target="InvertDiagBlocksLowerTriangular" | custom-call | tf_op jit(solution)/shard_map/jit(_solve_triangular)/triangular_solve | solution.py:767
  634.3 0.9 fusion.1.refs_8_
  635.1 10.5 %solve.1 = f32[64,256,128]{2,1,0:T(8,128)} custom-call(f32[32,32,256]{2,1,0:T(8,128)} %get-tuple-element.24.refs_0_, f32[32,32,256]{2,1,0:T(8,128)} %get-tuple-element.28.refs_1_, f32[32,32,256]{2,1,0:T(8,128)} %get-tuple-element.29.refs_2_, f32[32,32,256]{2,1,0:T(8,128)} %get-tuple-element.33.refs_3_, f32[32,32,256]{2,1,0:T(8,128)} %get-tuple-element.34.refs_4_, ...), custom_call_target="tpu_custom_call" | custom-call | tf_op jit(solution)/shard_map/solve/pallas_call | solution.py:722
  (9 shorter events, 0.1 us)
Async XLA Ops:
  1.5 78.2 %copy-start = (s32[256]{0:T(256)}, s32[256]{0:T(256)S(1)}, u32[]{:S(2)}) copy-start(s32[256]{0:T(256)S(1)} %sub.10.refs_0_) | copy-start | bytes 3076
  589.0 1.3 collective-permute-start
  590.3 4.3 collective-permute-start.1
  594.7 4.3 collective-permute-start.2
  599.0 6.3 collective-permute-start.3
  605.3 5.2 collective-permute-start.4

commit v3 on v2

--- a/solution.py
+++ b/solution.py
@@ -622,15 +622,84 @@
     return dict(zip(outs, results))
 
 
-def all_sum(x, axis):
-    n = lax.axis_size(axis)
-    if n & (n - 1):
-        return lax.psum(x, axis)
-    bit = 1
-    while bit < n:
-        x = x + lax.ppermute(x, axis, [(i, i ^ bit) for i in range(n)])
-        bit *= 2
-    return x
+def factor(gram, total_rows):
+    width = gram.shape[0]
+    rounds = []
+    for axis in ("row", "blk"):
+        size = lax.axis_size(axis)
+        if size & (size - 1):
+            gram = lax.psum(gram, axis)
+        else:
+            rounds += [(axis, 1 << b) for b in range(size.bit_length() - 1)]
+    count = len(rounds)
+    f32 = jnp.float32
+
+    def body(gram_ref, upper_ref, inverse_ref, sums, landed, left, right, send_sem, recv_sem):
+        def partner(axis, bit):
+            at = lax.axis_index(axis)
+            return {axis: at + bit * (1 - 2 * (at // bit % 2))}
+
+        barrier = pltpu.get_barrier_semaphore()
+        for axis, bit in rounds:
+            pl.semaphore_signal(barrier, inc=1, device_id=partner(axis, bit), device_id_type=MESH)
+        pl.semaphore_wait(barrier, count)
+
+        sums[0] = gram_ref[...]
+        for i, (axis, bit) in enumerate(rounds):
+            copy = pltpu.make_async_remote_copy(
+                src_ref=sums.at[i],
+                dst_ref=landed.at[i],
+                send_sem=send_sem.at[i],
+                recv_sem=recv_sem.at[i],
+                device_id=partner(axis, bit),
+                device_id_type=MESH,
+            )
+            copy.start()
+            copy.wait()
+            sums[i + 1] = sums[i] + landed[i]
+
+        shape = (width, width)
+        across = lax.broadcasted_iota(jnp.int32, shape, 0)
+        along = lax.broadcasted_iota(jnp.int32, shape, 1)
+        left[...] = sums[count] / total_rows
+        right[...] = jnp.where(across == along, 1.0, 0.0)
+
+        @pl.loop(0, width)
+        def _(j):
+            matrix = left[...]
+            picked = along == j
+            column = jnp.sum(jnp.where(picked, matrix, 0.0), axis=1, keepdims=True)
+            row = left[pl.ds(j, 1)]
+            other = right[pl.ds(j, 1)]
+            pivot = jnp.sum(jnp.where(picked[:1], row, 0.0), axis=1, keepdims=True)
+            scale = 1.0 / jnp.sqrt(pivot)
+            row = row * scale
+            other = other * scale
+            column = jnp.where(across[:, :1] > j, column * scale, 0.0)
+            here = across == j
+            left[...] = jnp.where(here, row, matrix - column * row)
+            right[...] = jnp.where(here, other, right[...] - column * other)
+
+        upper_ref[...] = jnp.where(along >= across, left[...], 0.0)
+        inverse_ref[...] = jnp.where(along <= across, right[...], 0.0)
+
+    square = pltpu.VMEM((width, width), f32)
+    return pl.pallas_call(
+        body,
+        out_shape=[jax.ShapeDtypeStruct((width, width), f32)] * 2,
+        in_specs=[pl.BlockSpec(memory_space=pltpu.VMEM)],
+        out_specs=[pl.BlockSpec(memory_space=pltpu.VMEM)] * 2,
+        scratch_shapes=[
+            pltpu.VMEM((count + 1, width, width), f32),
+            pltpu.VMEM((count, width, width), f32),
+            square,
+            square,
+            pltpu.SemaphoreType.DMA((count,)),
+            pltpu.SemaphoreType.DMA((count,)),
+        ],
+        compiler_params=pltpu.CompilerParams(collective_id=30, has_side_effects=True),
+        name="factor",
+    )(gram)
 
 
 def join(z_refs, early, b):
@@ -665,25 +734,27 @@
     batch = divisor(math.gcd(early, late), 8)
 
     def body(*refs):
-        *z_refs, out_ref, main, cross = refs
+        *z_refs, out_ref, total = refs
 
         @pl.when(pl.program_id(0) == 0)
         def _():
-            main[...] = jnp.zeros_like(main)
-            cross[...] = jnp.zeros_like(cross)
+            total[...] = jnp.zeros_like(total)
 
         for first in (True, False):
 
             @pl.when((pl.program_id(0) < early // batch) == first)
             def _(first=first):
+                part = None
                 for b in range(batch):
                     high, low = halves(join(z_refs, first, b))
-                    main[...] += outer(high, high)
-                    cross[...] += outer(high, low)
+                    term = outer(jnp.concatenate([high, low], axis=0), high)
+                    part = term if part is None else part + term
+                total[...] += part
 
         @pl.when(pl.program_id(0) == pl.num_programs(0) - 1)
         def _():
-            out_ref[...] = main[...] + (cross[...] + cross[...].T)
+            cross = total[width:]
+            out_ref[...] = total[:width] + (cross + cross.T)
 
     return pl.pallas_call(
         body,
@@ -691,7 +762,7 @@
         grid=((early + late) // batch,),
         in_specs=block_specs(pieces, batch, early // batch),
         out_specs=pl.BlockSpec((width, width), lambda i: (0, 0)),
-        scratch_shapes=[pltpu.VMEM((width, width), jnp.float32)] * 2,
+        scratch_shapes=[pltpu.VMEM((2 * width, width), jnp.float32)],
         name="gram",
     )(*pieces)
 
@@ -762,10 +833,8 @@
             pieces += [done["piece0"], done["piece1"]]
 
     total_rows = columns * side * lax.axis_size("row")
-    gram = all_sum(all_sum(gram_of(pieces), "row"), "blk") / total_rows
-    lower = jnp.linalg.cholesky(gram)
-    inverse = jax.scipy.linalg.solve_triangular(lower, jnp.eye(width, dtype=jnp.float32), lower=True)
-    return solve(pieces, inverse), lower.T
+    upper, inverse = factor(gram_of(pieces), total_rows)
+    return solve(pieces, inverse), upper
 
 
 def solution(mesh):

time: 647 us -> 637 us (0.985)
  Pallas kernels: 595 us -> 632 us
  other arithmetic: 24.4 us -> 1.47 us
  waiting for transfers between devices: 13 us -> 0 us
  starting transfers between devices: 8.5 us -> 0 us
    pallas_call x0 -> x1, Pallas kernels: none -> 37 us  [factor(): pl.pallas_call(body, out_shape=[jax.ShapeDtypeStruct((width, width), f32)...]
    another operation x4 -> x0, other arithmetic: 22.2 us -> none  [the longest x3 12.4 us: local(): lower = jnp.linalg.cholesky(gram)]
    ppermute x5 -> x0, waiting for transfers between devices: 13 us -> none  [all_sum(): x = x + lax.ppermute(x, axis, [(i, i ^ bit) for i in range(n)])]
    ppermute x5 -> x0, starting transfers between devices: 8.5 us -> none  [all_sum(): x = x + lax.ppermute(x, axis, [(i, i ^ bit) for i in range(n)])]
  transfers between devices with their start and end apart: 5 -> 0, of which waited for: 5 -> 0; matrix products, arithmetic and copies ran while one was open for 0% -> 0% of each run, Pallas kernels for 0% -> 0%
where the time goes in v3:
time: 637 us; the launch traced here: 636 us
  Pallas kernels  632 us (99%)
    pallas_call x4, Pallas kernels, stage(): pl.pallas_call(body, out_shape=list(outs.values()), in_specs=specs, out_s...  500 us
    pallas_call x1, Pallas kernels, gather(): pl.pallas_call(body, out_shape=[jax.ShapeDtypeStruct((n * blocks, wide, s...  76 us
    pallas_call x1, Pallas kernels, factor(): pl.pallas_call(body, out_shape=[jax.ShapeDtypeStruct((width, width), f32)...  37 us

profile of v3, /device:TPU:0, one launch (start us, length us, event | category | flops | bytes accessed | tf_op | source)
XLA Modules:
  0.0 636.2 jit_solution(7818137831339434178)
XLA Ops:
  0.6 0.7 broadcast_subtract_fusion
  1.3 0.1 copy.8
  1.4 0.1 sub.10.refs_0_
  1.5 0.0 copy-start.1
  1.5 0.2 select_reduce_fusion
  1.7 0.6 compare_select_fusion
  2.3 0.8 copy.9
  3.1 0.7 reshape.25.refs_1_
  3.8 76.0 %gather.1 = (bf16[256,32,256]{2,1,0:T(8,128)(2,1)}, bf16[64,32,256]{2,1,0:T(8,128)(2,1)}, bf16[64,32,256]{2,1,0:T(8,128)(2,1)}, bf16[64,32,256]{2,1,0:T(8,128)(2,1)}, bf16[64,32,256]{2,1,0:T(8,128)(2,1)}) custom-call(bf16[64,256,128]{2,1,0:T(8,128)(2,1)} %omega_ref.1), custom_call_target="tpu_custom_call" | custom-call | tf_op jit(solution)/shard_map/gather/pallas_call | solution.py:174
  79.7 0.0 copy-done.1
  79.7 114.1 %stage_0.1 = (f32[32,32,256]{2,1,0:T(8,128)}, bf16[256,32,256]{2,1,0:T(8,128)(2,1)}, f32[128,32,256]{2,1,0:T(8,128)}) custom-call(s32[256]{0:T(256)} %copy-done.1, f32[256]{0:T(256)} %reshape.25.refs_1_, s32[256]{0:T(256)} %get-tuple-element.47.refs_2_, s32[256]{0:T(256)} %get-tuple-element.46.refs_3_, bf16[64,4,256,256]{3,2,1,0:T(8,128)(2,1)} %refs_4_.7, ...), custom_call_target="tpu_custom_call" | custom-call | tf_op jit(solution)/shard_map/stage_0/pallas_call | solution.py:611
  193.9 127.8 %stage_1.1 = (f32[32,32,256]{2,1,0:T(8,128)}, bf16[256,32,256]{2,1,0:T(8,128)(2,1)}, f32[128,32,256]{2,1,0:T(8,128)}, f32[32,32,256]{2,1,0:T(8,128)}) custom-call(s32[256]{0:T(256)} %copy-done.1, f32[256]{0:T(256)} %reshape.25.refs_1_, s32[256]{0:T(256)} %get-tuple-element.47.refs_2_, s32[256]{0:T(256)} %get-tuple-element.46.refs_3_, ...), custom_call_target="tpu_custom_call" | custom-call | tf_op jit(solution)/shard_map/stage_1/pallas_call | solution.py:611
  321.7 127.0 %stage_2.1 = (f32[32,32,256]{2,1,0:T(8,128)}, bf16[256,32,256]{2,1,0:T(8,128)(2,1)}, f32[128,32,256]{2,1,0:T(8,128)}, f32[32,32,256]{2,1,0:T(8,128)}) custom-call(s32[256]{0:T(256)} %copy-done.1, f32[256]{0:T(256)} %reshape.25.refs_1_, s32[256]{0:T(256)} %get-tuple-element.47.refs_2_, s32[256]{0:T(256)} %get-tuple-element.46.refs_3_, ...), custom_call_target="tpu_custom_call" | custom-call | tf_op jit(solution)/shard_map/stage_2/pallas_call | solution.py:611
  448.7 131.1 %stage_3.1 = (f32[32,32,256]{2,1,0:T(8,128)}, f32[32,32,256]{2,1,0:T(8,128)}, f32[32,32,256]{2,1,0:T(8,128)}) custom-call(s32[256]{0:T(256)} %copy-done.1, f32[256]{0:T(256)} %reshape.25.refs_1_, s32[256]{0:T(256)} %get-tuple-element.47.refs_2_, s32[256]{0:T(256)} %get-tuple-element.46.refs_3_, bf16[64,4,256,256]{3,2,1,0:T(8,128)(2,1)} %refs_4_.7, ...), custom_call_target="tpu_custom_call" | custom-call | tf_op jit(solution)/shard_map/stage_3/pallas_call | solution.py:611
  579.8 8.3 %gram.1.gram_ref = f32[128,128]{1,0:T(8,128)} custom-call(f32[32,32,256]{2,1,0:T(8,128)} %get-tuple-element.26.refs_0_, f32[32,32,256]{2,1,0:T(8,128)} %get-tuple-element.30.refs_1_, f32[32,32,256]{2,1,0:T(8,128)} %get-tuple-element.31.refs_2_, f32[32,32,256]{2,1,0:T(8,128)} %get-tuple-element.35.refs_3_, f32[32,32,256]{2,1,0:T(8,128)} %get-tuple-element.36.refs_4_, ...), custom_call_target="tpu_custom_call" | custom-call | tf_op jit(solution)/shard_map/gram/pallas_call | solution.py:759
  588.1 37.0 %factor.1 = (f32[128,128]{1,0:T(8,128)}, f32[128,128]{1,0:T(8,128)}) custom-call(f32[128,128]{1,0:T(8,128)} %gram.1.gram_ref), custom_call_target="tpu_custom_call" | custom-call | tf_op jit(solution)/shard_map/factor/pallas_call | solution.py:687
  625.1 0.0 copy-start
  625.1 10.5 %solve.1 = f32[64,256,128]{2,1,0:T(8,128)} custom-call(f32[32,32,256]{2,1,0:T(8,128)} %get-tuple-element.26.refs_0_, f32[32,32,256]{2,1,0:T(8,128)} %get-tuple-element.30.refs_1_, f32[32,32,256]{2,1,0:T(8,128)} %get-tuple-element.31.refs_2_, f32[32,32,256]{2,1,0:T(8,128)} %get-tuple-element.35.refs_3_, f32[32,32,256]{2,1,0:T(8,128)} %get-tuple-element.36.refs_4_, ...), custom_call_target="tpu_custom_call" | custom-call | tf_op jit(solution)/shard_map/solve/pallas_call | solution.py:793
  635.6 0.0 copy-done
  635.6 0.6 copy.11
Async XLA Ops:
  1.5 78.2 %copy-start.1 = (s32[256]{0:T(256)}, s32[256]{0:T(256)S(1)}, u32[]{:S(2)}) copy-start(s32[256]{0:T(256)S(1)} %sub.10.refs_0_) | copy-start | bytes 3076
  625.1 10.5 %copy-start = (f32[128,128]{1,0:T(8,128)S(1)}, f32[128,128]{1,0:T(8,128)}, u32[]{:S(2)}) copy-start(f32[128,128]{1,0:T(8,128)} %get-tuple-element.51) | copy-start | bytes 196612

commit v4 on v3

--- a/solution.py
+++ b/solution.py
@@ -664,21 +664,44 @@
         left[...] = sums[count] / total_rows
         right[...] = jnp.where(across == along, 1.0, 0.0)
 
-        @pl.loop(0, width)
-        def _(j):
-            matrix = left[...]
-            picked = along == j
-            column = jnp.sum(jnp.where(picked, matrix, 0.0), axis=1, keepdims=True)
-            row = left[pl.ds(j, 1)]
-            other = right[pl.ds(j, 1)]
-            pivot = jnp.sum(jnp.where(picked[:1], row, 0.0), axis=1, keepdims=True)
-            scale = 1.0 / jnp.sqrt(pivot)
-            row = row * scale
-            other = other * scale
-            column = jnp.where(across[:, :1] > j, column * scale, 0.0)
-            here = across == j
-            left[...] = jnp.where(here, row, matrix - column * row)
-            right[...] = jnp.where(here, other, right[...] - column * other)
+        panel = divisor(width, 8)
+        down = lax.broadcasted_iota(jnp.int32, (panel, width), 0)
+        over = lax.broadcasted_iota(jnp.int32, (panel, width), 1)
+
+        @pl.loop(0, width // panel)
+        def _(q):
+            first = pl.multiple_of(q * panel, panel)
+            here = pl.ds(first, panel)
+            rows = [left[here], right[here]]
+            columns = [
+                jnp.broadcast_to(
+                    jnp.sum(jnp.where(over == first + t, rows[0], 0.0), axis=1, keepdims=True),
+                    (panel, width),
+                )
+                for t in range(panel)
+            ]
+            for t in range(panel):
+                scale = 1.0 / jnp.sqrt(columns[t][t : t + 1])
+                factors = jnp.where(down > t, columns[t] * scale, 0.0)
+
+                def pass_on(x, t=t, scale=scale, factors=factors):
+                    row = x[t : t + 1] * scale
+                    return jnp.where(down == t, row, x - factors * row)
+
+                columns = [pass_on(x) if u > t else x for u, x in enumerate(columns)]
+                rows = [pass_on(x) for x in rows]
+            below = jnp.where(along[:1] >= first + panel, rows[0], 0.0)
+            left[here] = rows[0]
+            right[here] = rows[1]
+            change = lax.dot_general(
+                below,
+                jnp.concatenate(rows, axis=1),
+                (((0,), (0,)), ((), ())),
+                precision=lax.Precision.HIGHEST,
+                preferred_element_type=f32,
+            )
+            left[...] = left[...] - change[:, :width]
+            right[...] = right[...] - change[:, width:]
 
         upper_ref[...] = jnp.where(along >= across, left[...], 0.0)
         inverse_ref[...] = jnp.where(along <= across, right[...], 0.0)

time: 637 us -> 631 us (level)
  no operation moved by 1% of the time
where the time goes in v4:
time: 631 us; the launch traced here: 630 us
  Pallas kernels  626 us (99%)
    pallas_call x4, Pallas kernels, stage(): pl.pallas_call(body, out_shape=list(outs.values()), in_specs=specs, out_s...  500 us
    pallas_call x1, Pallas kernels, gather(): pl.pallas_call(body, out_shape=[jax.ShapeDtypeStruct((n * blocks, wide, s...  76 us
    pallas_call x1, Pallas kernels, factor(): pl.pallas_call(body, out_shape=[jax.ShapeDtypeStruct((width, width), f32)...  30.8 us

profile of v4, /device:TPU:0, one launch (start us, length us, event | category | flops | bytes accessed | tf_op | source)
XLA Modules:
  0.0 630.1 jit_solution(4290844303313139265)
XLA Ops:
  0.6 0.7 broadcast_subtract_fusion
  1.3 0.1 copy.8
  1.4 0.1 sub.10.refs_0_
  1.5 0.0 copy-start.1
  1.5 0.2 select_reduce_fusion
  1.7 0.6 compare_select_fusion
  2.3 0.8 copy.9
  3.1 0.7 reshape.25.refs_1_
  3.8 76.0 %gather.1 = (bf16[256,32,256]{2,1,0:T(8,128)(2,1)}, bf16[64,32,256]{2,1,0:T(8,128)(2,1)}, bf16[64,32,256]{2,1,0:T(8,128)(2,1)}, bf16[64,32,256]{2,1,0:T(8,128)(2,1)}, bf16[64,32,256]{2,1,0:T(8,128)(2,1)}) custom-call(bf16[64,256,128]{2,1,0:T(8,128)(2,1)} %omega_ref.1), custom_call_target="tpu_custom_call" | custom-call | tf_op jit(solution)/shard_map/gather/pallas_call | solution.py:174
  79.7 0.0 copy-done.1
  79.7 114.1 %stage_0.1 = (f32[32,32,256]{2,1,0:T(8,128)}, bf16[256,32,256]{2,1,0:T(8,128)(2,1)}, f32[128,32,256]{2,1,0:T(8,128)}) custom-call(s32[256]{0:T(256)} %copy-done.1, f32[256]{0:T(256)} %reshape.25.refs_1_, s32[256]{0:T(256)} %get-tuple-element.47.refs_2_, s32[256]{0:T(256)} %get-tuple-element.46.refs_3_, bf16[64,4,256,256]{3,2,1,0:T(8,128)(2,1)} %refs_4_.7, ...), custom_call_target="tpu_custom_call" | custom-call | tf_op jit(solution)/shard_map/stage_0/pallas_call | solution.py:611
  193.9 127.8 %stage_1.1 = (f32[32,32,256]{2,1,0:T(8,128)}, bf16[256,32,256]{2,1,0:T(8,128)(2,1)}, f32[128,32,256]{2,1,0:T(8,128)}, f32[32,32,256]{2,1,0:T(8,128)}) custom-call(s32[256]{0:T(256)} %copy-done.1, f32[256]{0:T(256)} %reshape.25.refs_1_, s32[256]{0:T(256)} %get-tuple-element.47.refs_2_, s32[256]{0:T(256)} %get-tuple-element.46.refs_3_, ...), custom_call_target="tpu_custom_call" | custom-call | tf_op jit(solution)/shard_map/stage_1/pallas_call | solution.py:611
  321.7 127.0 %stage_2.1 = (f32[32,32,256]{2,1,0:T(8,128)}, bf16[256,32,256]{2,1,0:T(8,128)(2,1)}, f32[128,32,256]{2,1,0:T(8,128)}, f32[32,32,256]{2,1,0:T(8,128)}) custom-call(s32[256]{0:T(256)} %copy-done.1, f32[256]{0:T(256)} %reshape.25.refs_1_, s32[256]{0:T(256)} %get-tuple-element.47.refs_2_, s32[256]{0:T(256)} %get-tuple-element.46.refs_3_, ...), custom_call_target="tpu_custom_call" | custom-call | tf_op jit(solution)/shard_map/stage_2/pallas_call | solution.py:611
  448.7 131.1 %stage_3.1 = (f32[32,32,256]{2,1,0:T(8,128)}, f32[32,32,256]{2,1,0:T(8,128)}, f32[32,32,256]{2,1,0:T(8,128)}) custom-call(s32[256]{0:T(256)} %copy-done.1, f32[256]{0:T(256)} %reshape.25.refs_1_, s32[256]{0:T(256)} %get-tuple-element.47.refs_2_, s32[256]{0:T(256)} %get-tuple-element.46.refs_3_, bf16[64,4,256,256]{3,2,1,0:T(8,128)(2,1)} %refs_4_.7, ...), custom_call_target="tpu_custom_call" | custom-call | tf_op jit(solution)/shard_map/stage_3/pallas_call | solution.py:611
  579.8 8.3 %gram.1.gram_ref = f32[128,128]{1,0:T(8,128)} custom-call(f32[32,32,256]{2,1,0:T(8,128)} %get-tuple-element.26.refs_0_, f32[32,32,256]{2,1,0:T(8,128)} %get-tuple-element.30.refs_1_, f32[32,32,256]{2,1,0:T(8,128)} %get-tuple-element.31.refs_2_, f32[32,32,256]{2,1,0:T(8,128)} %get-tuple-element.35.refs_3_, f32[32,32,256]{2,1,0:T(8,128)} %get-tuple-element.36.refs_4_, ...), custom_call_target="tpu_custom_call" | custom-call | tf_op jit(solution)/shard_map/gram/pallas_call | solution.py:782
  588.1 30.8 %factor.1 = (f32[128,128]{1,0:T(8,128)}, f32[128,128]{1,0:T(8,128)}) custom-call(f32[128,128]{1,0:T(8,128)} %gram.1.gram_ref), custom_call_target="tpu_custom_call" | custom-call | tf_op jit(solution)/shard_map/factor/pallas_call | solution.py:710
  618.9 0.0 copy-start
  618.9 10.5 %solve.1 = f32[64,256,128]{2,1,0:T(8,128)} custom-call(f32[32,32,256]{2,1,0:T(8,128)} %get-tuple-element.26.refs_0_, f32[32,32,256]{2,1,0:T(8,128)} %get-tuple-element.30.refs_1_, f32[32,32,256]{2,1,0:T(8,128)} %get-tuple-element.31.refs_2_, f32[32,32,256]{2,1,0:T(8,128)} %get-tuple-element.35.refs_3_, f32[32,32,256]{2,1,0:T(8,128)} %get-tuple-element.36.refs_4_, ...), custom_call_target="tpu_custom_call" | custom-call | tf_op jit(solution)/shard_map/solve/pallas_call | solution.py:816
  629.4 0.0 copy-done
  629.4 0.6 copy.11
Async XLA Ops:
  1.5 78.2 %copy-start.1 = (s32[256]{0:T(256)}, s32[256]{0:T(256)S(1)}, u32[]{:S(2)}) copy-start(s32[256]{0:T(256)S(1)} %sub.10.refs_0_) | copy-start | bytes 3076
  618.9 10.5 %copy-start = (f32[128,128]{1,0:T(8,128)S(1)}, f32[128,128]{1,0:T(8,128)}, u32[]{:S(2)}) copy-start(f32[128,128]{1,0:T(8,128)} %get-tuple-element.51) | copy-start | bytes 196612

commit v5 on v2

--- a/solution.py
+++ b/solution.py
@@ -11,6 +11,7 @@
 LEVELS = 32767.0
 TINY = 1e-30
 HOP = 2
+LEAD = 8
 ANY = pl.BlockSpec(memory_space=pl.ANY)
 SMEM = pl.BlockSpec(memory_space=pltpu.SMEM)
 
@@ -38,8 +39,10 @@
     return code.astype(jnp.int32).astype(jnp.float32) * column
 
 
-def greet(me, n):
+def greet(me, n, rounds=()):
     barrier = pltpu.get_barrier_semaphore()
+    for axis, bit in rounds:
+        pl.semaphore_signal(barrier, inc=1, device_id=partner(axis, bit), device_id_type=MESH)
 
     @pl.when(me > 0)
     def _():
@@ -50,7 +53,7 @@
         pl.semaphore_signal(barrier, inc=1, device_id={"blk": me + 1}, device_id_type=MESH)
 
     peers = jnp.where(me > 0, 1, 0) + jnp.where(me < n - 1, 1, 0)
-    pl.semaphore_wait(barrier, peers)
+    pl.semaphore_wait(barrier, peers + len(rounds))
 
 
 def gather_steps(me, n, base, count, size, own_ref, slab_ref, send_sem, recv_sem):
@@ -269,7 +272,238 @@
     return step, start + max([reach] + [hop * b + (n - b) * pieces for b in range(1, n)]), finish
 
 
-def stage(part, values, own, slab, tables, n, following=None, rest=None):
+def halves(x):
+    high = x.astype(jnp.bfloat16)
+    return high, (x - high.astype(jnp.float32)).astype(jnp.bfloat16)
+
+
+def outer(x, y):
+    return lax.dot_general(x, y, (((1,), (1,)), ((), ())), preferred_element_type=jnp.float32)
+
+
+def exact(x, y, a, b):
+    return lax.dot_general(
+        x,
+        y,
+        (((a,), (b,)), ((), ())),
+        precision=lax.Precision.HIGHEST,
+        preferred_element_type=jnp.float32,
+    )
+
+
+def rounds_of():
+    rounds = []
+    for axis in ("row", "blk"):
+        size = lax.axis_size(axis)
+        assert size & (size - 1) == 0
+        rounds += [(axis, 1 << b) for b in range(size.bit_length() - 1)]
+    return rounds
+
+
+def partner(axis, bit):
+    at = lax.axis_index(axis)
+    return {axis: at + bit * (1 - 2 * (at // bit % 2))}
+
+
+def exchange(i, axis, bit, sums, landed, send_sem, recv_sem):
+    return pltpu.make_async_remote_copy(
+        src_ref=sums.at[i],
+        dst_ref=landed.at[i],
+        send_sem=send_sem.at[i],
+        recv_sem=recv_sem.at[i],
+        device_id=partner(axis, bit),
+        device_id_type=MESH,
+    )
+
+
+def eliminate(left, right):
+    height, width = left.shape
+    panel = divisor(height, 8)
+    down = lax.broadcasted_iota(jnp.int32, (panel, width), 0)
+    over = lax.broadcasted_iota(jnp.int32, (panel, width), 1)
+
+    def step(q):
+        first = pl.multiple_of(q * panel, panel)
+        here = pl.ds(first, panel)
+        rows = [left[here], right[here]]
+        columns = [
+            jnp.broadcast_to(
+                jnp.sum(jnp.where(over == first + t, rows[0], 0.0), axis=1, keepdims=True),
+                (panel, width),
+            )
+            for t in range(panel)
+        ]
+        for t in range(panel):
+            scale = 1.0 / jnp.sqrt(columns[t][t : t + 1])
+            factors = jnp.where(down > t, columns[t] * scale, 0.0)
+
+            def pass_on(x, t=t, scale=scale, factors=factors):
+                row = x[t : t + 1] * scale
+                return jnp.where(down == t, row, x - factors * row)
+
+            columns = [pass_on(x) if u > t else x for u, x in enumerate(columns)]
+            rows = [pass_on(x) for x in rows]
+        below = jnp.where(over >= first + panel, rows[0], 0.0)
+        left[here] = rows[0]
+        right[here] = rows[1]
+        left[...] = left[...] - exact(below, rows[0], 0, 0)[:height]
+        right[...] = right[...] - exact(below, rows[1], 0, 0)[:height]
+
+    return step, height // panel
+
+
+def known_gram(g, sources, now_size, now, half, wide, side, width, total_rows, mine, rounds, final):
+    q = len(sources[0])
+    known = q * wide
+    chunks = now // now_size
+    early_chunks = half // now_size
+    buffer, total, sums, landed = g["zbuf"], g["total"], g["gram_sums"], g["gram_landed"]
+    left, right = g["left"], g["right"]
+    tail_sums, tail_landed, cross = g["tail_sums"], g["tail_landed"], g["tail_sums"].at[0]
+    f32 = jnp.float32
+
+    def load(c, p, late):
+        at = (c - early_chunks if late else c) * now_size
+        return pltpu.make_async_copy(
+            sources[1 if late else 0][p].at[pl.ds(at, now_size)],
+            buffer.at[c % 2, p],
+            g["zbuf_sem"].at[c % 2, p],
+        )
+
+    def fetch(c):
+        for late in (False, True):
+
+            @pl.when((c >= early_chunks) == late)
+            def _(late=late):
+                for p in range(q):
+                    load(c, p, late).start()
+
+    def ready(c):
+        for p in range(q):
+            pltpu.make_async_copy(
+                sources[0][p].at[pl.ds(0, now_size)], buffer.at[c % 2, p], g["zbuf_sem"].at[c % 2, p]
+            ).wait()
+
+    def follow(c):
+        @pl.when(c + 1 < chunks)
+        def _():
+            fetch(c + 1)
+
+        ready(c)
+
+    def inner(c):
+        follow(c)
+        part = None
+        blank = jnp.zeros((width - known, side), jnp.bfloat16)
+        for b in range(now_size):
+            z = jnp.concatenate([buffer[c % 2, p, b] for p in range(q)], axis=0)
+            high, low = halves(z)
+            term = outer(
+                jnp.concatenate([high, low], axis=0), jnp.concatenate([high, blank], axis=0)
+            )
+            part = term if part is None else part + term
+        total[...] += part
+
+    def rows_of(c):
+        follow(c)
+        part = None
+        for b in range(now_size):
+            z = [buffer[c % 2, p, b] for p in range(q)] + [mine[c * now_size + b]]
+            high, low = halves(jnp.concatenate(z, axis=0))
+            both = outer(jnp.concatenate([high[known:], low[known:]], axis=0), high)
+            term = both[:wide] + both[wide:] + outer(high[known:], low)
+            part = term if part is None else part + term
+        cross[...] += part
+
+    count = len(rounds)
+    panel_step, panels = eliminate(left, right)
+    per_tick = 3
+    solved = chunks + count + 1
+    start = max(final, solved + -(-panels // per_tick))
+
+    def begin():
+        total[...] = jnp.zeros((2 * known, width), f32)
+        cross[...] = jnp.zeros((wide, width), f32)
+        fetch(0)
+
+    def copy(i):
+        return exchange(i, *rounds[i], sums, landed, g["gram_send"], g["gram_recv"])
+
+    def step(s):
+        @pl.when(s < chunks)
+        def _():
+            inner(s)
+
+        for i in range(count + 1):
+
+            @pl.when(s == chunks + i)
+            def _(i=i):
+                if i == 0:
+                    low = total[known:]
+                    square = jnp.concatenate([low, jnp.zeros((width - known, width), f32)], axis=0)
+                    sums[0] = total[:known] + (low + square.T[:known])
+                else:
+                    copy(i - 1).wait()
+                    sums[i] = sums[i - 1] + landed[i - 1]
+                if i < count:
+                    copy(i).start()
+                else:
+                    across = lax.broadcasted_iota(jnp.int32, (known, width), 0)
+                    along = lax.broadcasted_iota(jnp.int32, (known, width), 1)
+                    left[...] = sums[count] / total_rows
+                    right[...] = jnp.where(across == along, 1.0, 0.0)
+
+        for j in range(per_tick):
+            panel = (s - solved) * per_tick + j
+
+            @pl.when((s >= solved) & (panel < panels))
+            def _(panel=panel):
+                panel_step(panel)
+
+        @pl.when(s == start - 1)
+        def _():
+            fetch(0)
+
+        @pl.when(s >= start)
+        def _():
+            rows_of(s - start)
+
+    def end():
+        upper, inverse, corner_left, corner_right = (
+            g[k] for k in ("upper_ref", "inverse_ref", "corner_left", "corner_right")
+        )
+        for i, (axis, bit) in enumerate(rounds):
+            copy = exchange(i, axis, bit, tail_sums, tail_landed, g["tail_send"], g["tail_recv"])
+            copy.start()
+            if i == 0:
+                across = lax.broadcasted_iota(jnp.int32, (known, width), 0)
+                along = lax.broadcasted_iota(jnp.int32, (known, width), 1)
+                blank = jnp.zeros((width - known, width), f32)
+                upper[:known] = jnp.where(along >= across, left[...], 0.0)
+                inverse[:known] = jnp.where(along <= across, right[...], 0.0)
+                upper[known:] = blank
+                inverse[known:] = blank
+            copy.wait()
+            tail_sums[i + 1] = tail_sums[i] + tail_landed[i]
+        mixed = tail_sums[count] / total_rows
+        head = inverse[...]
+        turned = exact(mixed, head, 1, 1)
+        corner_left[...] = mixed[:, known:] - exact(turned, turned, 1, 1)
+        across = lax.broadcasted_iota(jnp.int32, (wide, wide), 0)
+        along = lax.broadcasted_iota(jnp.int32, (wide, wide), 1)
+        corner_right[...] = jnp.where(across == along, 1.0, 0.0)
+        corner_step, corner_panels = eliminate(corner_left, corner_right)
+        pl.loop(0, corner_panels)(corner_step)
+        last_inverse = jnp.where(along <= across, corner_right[...], 0.0)
+        upper[:known, known:] = turned.T[:known]
+        upper[known:, known:] = jnp.where(along >= across, corner_left[...], 0.0)
+        inverse[known:, :] = -exact(last_inverse, exact(turned, head, 1, 0), 1, 0)
+        inverse[known:, known:] = last_inverse
+
+    return begin, step, start + chunks, end
+
+
+def stage(part, values, own, slab, tables, n, following=None, rest=None, sources=None, total_rows=0):
     rows, per, side, _ = values.shape
     blocks, wide, _ = own.shape
     lanes = 128
@@ -282,7 +516,8 @@
     half = blocks // 2
     late = blocks - half
     now = half if following is not None else blocks
-    now_size = divisor(now, 4 if following is not None else 8)
+    now_size = divisor(now, 4) if following is not None else divisor(math.gcd(half, late), 8)
+    rounds = rounds_of() if following is None else []
     late_size = divisor(late, 4)
     gather_size = divisor(half, 4)
     f32 = jnp.float32
@@ -338,6 +573,32 @@
             zs=pltpu.VMEM((n * late, wide, side), f32),
             zs_sem=pltpu.SemaphoreType.DMA(()),
         )
+    out_specs = [ANY] * len(outs)
+    if following is None:
+        q = (len(sources) + 1) // 2
+        known, width = q * wide, (q + 1) * wide
+        args.update({f"source{i}": x for i, x in enumerate(sources)})
+        specs += [ANY] * len(sources)
+        square = jax.ShapeDtypeStruct((width, width), f32)
+        outs.update(upper=square, inverse=square)
+        out_specs += [pl.BlockSpec(memory_space=pltpu.VMEM)] * 2
+        scratch.update(
+            zbuf=pltpu.VMEM((2, q, now_size, wide, side), f32),
+            zbuf_sem=pltpu.SemaphoreType.DMA((2, q)),
+            total=pltpu.VMEM((2 * known, width), f32),
+            gram_sums=pltpu.VMEM((len(rounds) + 1, known, width), f32),
+            gram_landed=pltpu.VMEM((len(rounds), known, width), f32),
+            left=pltpu.VMEM((known, width), f32),
+            right=pltpu.VMEM((known, width), f32),
+            tail_sums=pltpu.VMEM((len(rounds) + 1, wide, width), f32),
+            tail_landed=pltpu.VMEM((len(rounds), wide, width), f32),
+            corner_left=pltpu.VMEM((wide, wide), f32),
+            corner_right=pltpu.VMEM((wide, wide), f32),
+            tail_send=pltpu.SemaphoreType.DMA((len(rounds),)),
+            tail_recv=pltpu.SemaphoreType.DMA((len(rounds),)),
+            gram_send=pltpu.SemaphoreType.DMA((len(rounds),)),
+            gram_recv=pltpu.SemaphoreType.DMA((len(rounds),)),
+        )
     names = list(args) + list(outs) + list(scratch)
     names[len(args) : len(args) + len(outs)] = [f"{name}_ref" for name in outs]
     names[: len(args)] = [f"{name}_ref" for name in args]
@@ -379,7 +640,7 @@
         if rest is not None:
             zs_copy = pltpu.make_async_copy(g["rest_ref"], g["zs"], g["zs_sem"])
             zs_copy.start()
-        greet(me, n)
+        greet(me, n, rounds)
         sums[items] = jnp.zeros((wide, side), f32)
 
         @pl.when(me == 0)
@@ -397,7 +658,7 @@
                 me, n, 0, half, gather_size, g["following_ref"], g["following_slab_ref"],
                 *(g[k] for k in early_names),
             )
-            lead = min(2, steps)
+            lead = min(LEAD, half // gather_size)
             extra.append((lambda s, step=step: step(s + lead), steps - lead))
             ends.append(finish)
             for v in range(lead):
@@ -411,7 +672,7 @@
             step, steps, finish = reduce_steps(
                 me, n, late, late_size, eye, read_rest, zs, me * late,
                 [g[k] for k in late_names], following is not None,
-                max(half // gather_size - 2, 0) if following is not None else 0,
+                max(half // gather_size - LEAD, 0) if following is not None else 0,
             )
             extra.append((step, steps))
             ends.append(finish)
@@ -544,6 +805,18 @@
         )
         second = [(step, steps)]
         ends.append(finish)
+        if following is None:
+            rest_copy.wait()
+            early = [g[f"source{2 * i}_ref"] for i in range(q)]
+            late_refs = [g[f"source{2 * i + 1}_ref"] for i in range(q - 1)]
+            late_refs.append(g["rest_piece_ref"])
+            share = now // now_size
+            begin, step, steps, close = known_gram(
+                g, (early, late_refs), now_size, now, half, wide, side, width, total_rows, mine,
+                rounds, max(HOP + (n - 2) * share, HOP * (n - 1)),
+            )
+            begin()
+            second.append((step, steps))
         if following is not None:
             second.append((lambda s: late_step(s + ahead), late_steps - ahead))
             shelf = g["shelf"]
@@ -585,6 +858,8 @@
         ]
         for one in mine_copies:
             one.start()
+        if following is None:
+            close()
 
         @pl.loop(0, pieces)
         def _(c):
@@ -603,7 +878,7 @@
         if following is not None:
             for i in range(max(shelves - 2, 0), shelves):
                 store(i).wait()
-        if rest is not None:
+        if rest is not None and following is not None:
             rest_copy.wait()
         for one in mine_copies:
             one.wait()
@@ -612,7 +887,7 @@
         body,
         out_shape=list(outs.values()),
         in_specs=specs,
-        out_specs=[ANY] * len(outs),
+        out_specs=out_specs,
         scratch_shapes=list(scratch.values()),
         compiler_params=pltpu.CompilerParams(
             collective_id=2 + part, has_side_effects=True, vmem_limit_bytes=63 << 20
@@ -620,17 +895,6 @@
         name=f"stage_{part}",
     )(*args.values())
     return dict(zip(outs, results))
-
-
-def all_sum(x, axis):
-    n = lax.axis_size(axis)
-    if n & (n - 1):
-        return lax.psum(x, axis)
-    bit = 1
-    while bit < n:
-        x = x + lax.ppermute(x, axis, [(i, i ^ bit) for i in range(n)])
-        bit *= 2
-    return x
 
 
 def join(z_refs, early, b):
@@ -649,53 +913,6 @@
     return specs
 
 
-def halves(x):
-    high = x.astype(jnp.bfloat16)
-    return high, (x - high.astype(jnp.float32)).astype(jnp.bfloat16)
-
-
-def outer(x, y):
-    return lax.dot_general(x, y, (((1,), (1,)), ((), ())), preferred_element_type=jnp.float32)
-
-
-def gram_of(pieces):
-    early, late = pieces[0].shape[0], pieces[1].shape[0]
-    side = pieces[0].shape[2]
-    width = sum(piece.shape[1] for piece in pieces[::2])
-    batch = divisor(math.gcd(early, late), 8)
-
-    def body(*refs):
-        *z_refs, out_ref, main, cross = refs
-
-        @pl.when(pl.program_id(0) == 0)
-        def _():
-            main[...] = jnp.zeros_like(main)
-            cross[...] = jnp.zeros_like(cross)
-
-        for first in (True, False):
-
-            @pl.when((pl.program_id(0) < early // batch) == first)
-            def _(first=first):
-                for b in range(batch):
-                    high, low = halves(join(z_refs, first, b))
-                    main[...] += outer(high, high)
-                    cross[...] += outer(high, low)
-
-        @pl.when(pl.program_id(0) == pl.num_programs(0) - 1)
-        def _():
-            out_ref[...] = main[...] + (cross[...] + cross[...].T)
-
-    return pl.pallas_call(
-        body,
-        out_shape=jax.ShapeDtypeStruct((width, width), jnp.float32),
-        grid=((early + late) // batch,),
-        in_specs=block_specs(pieces, batch, early // batch),
-        out_specs=pl.BlockSpec((width, width), lambda i: (0, 0)),
-        scratch_shapes=[pltpu.VMEM((width, width), jnp.float32)] * 2,
-        name="gram",
-    )(*pieces)
-
-
 def crossed(x, y):
     return lax.dot_general(x, y, (((0,), (1,)), ((), ())), preferred_element_type=jnp.float32)
 
@@ -714,10 +931,11 @@
 
             @pl.when((pl.program_id(0) < early // batch) == first)
             def _(first=first):
-                for b in range(batch):
-                    high, low = halves(join(z_refs, first, b))
-                    both = jnp.concatenate([high, low], axis=0)
-                    out_ref[b] = crossed(both, inv_twice) + crossed(high, inv_low)
+                z = jnp.concatenate([join(z_refs, first, b) for b in range(batch)], axis=1)
+                high, low = halves(z)
+                both = jnp.concatenate([high, low], axis=0)
+                out = crossed(both, inv_twice) + crossed(high, inv_low)
+                out_ref[...] = out.reshape(batch, side, width)
 
     return pl.pallas_call(
         body,
@@ -747,12 +965,16 @@
     last = jnp.where(last < 0, items, last)
 
     parts = 4
+    total_rows = columns * side * lax.axis_size("row")
     slab, *own = gather(omega, n, parts)
     rest = None
     pieces = []
     for p in range(parts):
         following = own[p + 1] if p + 1 < parts else None
-        done = stage(p, values, own[p], slab, (cols, weights, prev, last), n, following, rest)
+        done = stage(
+            p, values, own[p], slab, (cols, weights, prev, last), n, following, rest,
+            pieces if following is None else None, total_rows,
+        )
         if p:
             pieces.append(done["rest_piece"])
         if p + 1 < parts:
@@ -761,11 +983,7 @@
         else:
             pieces += [done["piece0"], done["piece1"]]
 
-    total_rows = columns * side * lax.axis_size("row")
-    gram = all_sum(all_sum(gram_of(pieces), "row"), "blk") / total_rows
-    lower = jnp.linalg.cholesky(gram)
-    inverse = jax.scipy.linalg.solve_triangular(lower, jnp.eye(width, dtype=jnp.float32), lower=True)
-    return solve(pieces, inverse), lower.T
+    return solve(pieces, done["inverse"]), done["upper"]
 
 
 def solution(mesh):

time: 647 us -> 607 us (0.938)
  other arithmetic: 24.4 us -> 1.47 us
  waiting for transfers between devices: 13 us -> 0 us
  starting transfers between devices: 8.5 us -> 0 us
    another operation x4 -> x0, other arithmetic: 22.2 us -> none  [the longest x3 12.4 us: local(): lower = jnp.linalg.cholesky(gram)]
    pallas_call x4, Pallas kernels: 500 us -> 514 us  [stage(): pl.pallas_call(body, out_shape=list(outs.values()), in_specs=specs, out_s...]
    ppermute x5 -> x0, waiting for transfers between devices: 13 us -> none  [all_sum(): x = x + lax.ppermute(x, axis, [(i, i ^ bit) for i in range(n)])]
    ppermute x5 -> x0, starting transfers between devices: 8.5 us -> none  [all_sum(): x = x + lax.ppermute(x, axis, [(i, i ^ bit) for i in range(n)])]
    pallas_call x1 -> x0, Pallas kernels: 8.31 us -> none  [gram_of(): pl.pallas_call(body, out_shape=jax.ShapeDtypeStruct((width, width), jnp.f...]
  transfers between devices with their start and end apart: 5 -> 0, of which waited for: 5 -> 0; matrix products, arithmetic and copies ran while one was open for 0% -> 0% of each run, Pallas kernels for 0% -> 0%
where the time goes in v5:
time: 607 us; the launch traced here: 605 us
  Pallas kernels  601 us (99%)
    pallas_call x4, Pallas kernels, stage(): pl.pallas_call(body, out_shape=list(outs.values()), in_specs=specs, out_s...  514 us
    pallas_call x1, Pallas kernels, gather(): pl.pallas_call(body, out_shape=[jax.ShapeDtypeStruct((n * blocks, wide, s...  76 us

profile of v5, /device:TPU:0, one launch (start us, length us, event | category | flops | bytes accessed | tf_op | source)
XLA Modules:
  0.0 605.4 jit_solution(18278972948603062712)
XLA Ops:
  0.6 0.7 broadcast_subtract_fusion
  1.3 0.1 copy.8
  1.4 0.1 sub.10.refs_0_
  1.5 0.0 copy-start.1
  1.5 0.2 select_reduce_fusion
  1.7 0.6 compare_select_fusion
  2.3 0.8 copy.9
  3.1 0.7 reshape.25.refs_1_
  3.8 76.0 %gather.1 = (bf16[256,32,256]{2,1,0:T(8,128)(2,1)}, bf16[64,32,256]{2,1,0:T(8,128)(2,1)}, bf16[64,32,256]{2,1,0:T(8,128)(2,1)}, bf16[64,32,256]{2,1,0:T(8,128)(2,1)}, bf16[64,32,256]{2,1,0:T(8,128)(2,1)}) custom-call(bf16[64,256,128]{2,1,0:T(8,128)(2,1)} %omega_ref.1), custom_call_target="tpu_custom_call" | custom-call | tf_op jit(solution)/shard_map/gather/pallas_call | solution.py:177
  79.7 0.0 copy-done.1
  79.7 111.9 %stage_0.1 = (f32[32,32,256]{2,1,0:T(8,128)}, bf16[256,32,256]{2,1,0:T(8,128)(2,1)}, f32[128,32,256]{2,1,0:T(8,128)}) custom-call(s32[256]{0:T(256)} %copy-done.1, f32[256]{0:T(256)} %reshape.25.refs_1_, s32[256]{0:T(256)} %get-tuple-element.47.refs_2_, s32[256]{0:T(256)} %get-tuple-element.46.refs_3_, bf16[64,4,256,256]{3,2,1,0:T(8,128)(2,1)} %refs_4_.7, ...), custom_call_target="tpu_custom_call" | custom-call | tf_op jit(solution)/shard_map/stage_0/pallas_call | solution.py:886
  191.7 125.1 %stage_1.1 = (f32[32,32,256]{2,1,0:T(8,128)}, bf16[256,32,256]{2,1,0:T(8,128)(2,1)}, f32[128,32,256]{2,1,0:T(8,128)}, f32[32,32,256]{2,1,0:T(8,128)}) custom-call(s32[256]{0:T(256)} %copy-done.1, f32[256]{0:T(256)} %reshape.25.refs_1_, s32[256]{0:T(256)} %get-tuple-element.47.refs_2_, s32[256]{0:T(256)} %get-tuple-element.46.refs_3_, ...), custom_call_target="tpu_custom_call" | custom-call | tf_op jit(solution)/shard_map/stage_1/pallas_call | solution.py:886
  316.8 123.7 %stage_2.1 = (f32[32,32,256]{2,1,0:T(8,128)}, bf16[256,32,256]{2,1,0:T(8,128)(2,1)}, f32[128,32,256]{2,1,0:T(8,128)}, f32[32,32,256]{2,1,0:T(8,128)}) custom-call(s32[256]{0:T(256)} %copy-done.1, f32[256]{0:T(256)} %reshape.25.refs_1_, s32[256]{0:T(256)} %get-tuple-element.47.refs_2_, s32[256]{0:T(256)} %get-tuple-element.46.refs_3_, ...), custom_call_target="tpu_custom_call" | custom-call | tf_op jit(solution)/shard_map/stage_2/pallas_call | solution.py:886
  440.5 153.7 %stage_3.1 = (f32[32,32,256]{2,1,0:T(8,128)}, f32[32,32,256]{2,1,0:T(8,128)}, f32[32,32,256]{2,1,0:T(8,128)}, f32[128,128]{1,0:T(8,128)}, f32[128,128]{1,0:T(8,128)}) custom-call(s32[256]{0:T(256)} %copy-done.1, f32[256]{0:T(256)} %reshape.25.refs_1_, s32[256]{0:T(256)} %get-tuple-element.47.refs_2_, s32[256]{0:T(256)} %get-tuple-element.46.refs_3_, ...), custom_call_target="tpu_custom_call" | custom-call | tf_op jit(solution)/shard_map/stage_3/pallas_call | solution.py:886
  594.2 0.0 copy-start
  594.3 10.5 %solve.1 = f32[64,256,128]{2,1,0:T(8,128)} custom-call(f32[32,32,256]{2,1,0:T(8,128)} %get-tuple-element.26.refs_8_.refs_0_, f32[32,32,256]{2,1,0:T(8,128)} %get-tuple-element.30.refs_9_.refs_1_, f32[32,32,256]{2,1,0:T(8,128)} %get-tuple-element.31.refs_10_.refs_2_, f32[32,32,256]{2,1,0:T(8,128)} %get-tuple-element.35.refs_11_.refs_3_, ...), custom_call_target="tpu_custom_call" | custom-call | tf_op jit(solution)/shard_map/solve/pallas_call | solution.py:940
  604.8 0.0 copy-done
  604.8 0.6 copy.11
Async XLA Ops:
  1.5 78.2 %copy-start.1 = (s32[256]{0:T(256)}, s32[256]{0:T(256)S(1)}, u32[]{:S(2)}) copy-start(s32[256]{0:T(256)S(1)} %sub.10.refs_0_) | copy-start | bytes 3076
  594.2 10.5 %copy-start = (f32[128,128]{1,0:T(8,128)S(1)}, f32[128,128]{1,0:T(8,128)}, u32[]{:S(2)}) copy-start(f32[128,128]{1,0:T(8,128)} %get-tuple-element.51) | copy-start | bytes 196612
